TPU v7x, 256 devices: a whole 4x4x8 slice. The times are simulated.
256 devices in a mesh: ctx: 32 (over y, z), head: 8 (over x, core).
Axes of the slice: x: 4, y: 4, z: 8, core: 2. Of those that a mesh axis runs over, the one named last changes fastest.
Arguments:
- lin_q: bfloat16 [4096, 32, 128], P('ctx', 'head'), may hold values from -4 to 4
- lin_k: bfloat16 [4096, 32, 128], P('ctx', 'head'), may hold values from -4 to 4
- lin_v: bfloat16 [4096, 32, 128], P('ctx', 'head'), may hold values from -16 to 16
- lin_decay: float32 [32, 4096], P('head', 'ctx'), may hold values from -1.5 to 0
- norm_gain: float32 [32, 128], P('head'), may hold values from 0.1 to 1.9
- soft_q: bfloat16 [4096, 32, 128], P('ctx', 'head'), may hold values from -5 to 5
- soft_k: bfloat16 [4096, 32, 128], P('ctx', 'head'), may hold values from -5 to 5
- soft_v: bfloat16 [4096, 32, 128], P('ctx', 'head'), may hold values from -5 to 5
- out_grad: bfloat16 [4096, 32, 128], P('ctx', 'head'), may hold values from -5 to 5
- block_lists: int32 [32, 16], P('ctx'), may hold values from 0 to 30, as said below
- block_counts: int32 [32], P('ctx'), may hold values from 0 to 16, as said below
Outputs:
- lin_dq: bfloat16 [4096, 32, 128], P('ctx', 'head')
- lin_dk: bfloat16 [4096, 32, 128], P('ctx', 'head')
- lin_dv: bfloat16 [4096, 32, 128], P('ctx', 'head')
- soft_dq: bfloat16 [4096, 32, 128], P('ctx', 'head')
- soft_dk: bfloat16 [4096, 32, 128], P('ctx', 'head')
- soft_dv: bfloat16 [4096, 32, 128], P('ctx', 'head')
Inputs may be any that keep to these rules, and one draw needn't show every extreme that they name: `block_lists`: entries past block_counts[b] are 0. The first block_counts[b] entries of query block b are distinct blocks that lie before the span of 128 tokens holding b. All query blocks of one span name together at most one block of each other span. In every span after the first, some query block names every block that its span names; from the second span on these include block 0, and from the third on also the last block before the span. `block_counts`: in span i of 128 tokens some query block has the count min(i, 16); every count is at most that; counts are 0 only in the first span.
All inputs are finite; a program needn't handle non-finite values.
Results may differ from a plain program's by a relative error of at most 0.011.
Values may be sent and summed in bfloat16 or wider, within the bound.
A program may use at most 128 MiB of HBM per device.

v0:
```python
import jax
import jax.numpy as jnp
from jax import lax
from jax.sharding import PartitionSpec as P

BLK = 128
NSEL = 16


epsilon = 1e-05
exact_precision = lax.Precision.HIGHEST


def carried_in(part, axis, combine, identity, reverse):
    count = lax.axis_size(axis)
    place = lax.axis_index(axis)
    ahead = count - 1 - place if reverse else place
    gathered = jax.tree.map(lambda a: lax.all_gather(a, axis), part)
    state = jax.tree.map(lambda a, e: jnp.zeros_like(a) + jnp.asarray(e, a.dtype), part, identity)

    def one(lap, state):
        source = count - 1 - lap if reverse else lap
        return combine(
            state, jax.tree.map(lambda a: lax.dynamic_index_in_dim(a, source, 0, False), gathered)
        )

    return lax.fori_loop(0, ahead, one, state)


def decay_tables(decays):
    running = jnp.cumsum(decays, axis=1)
    finish = running[:, -1]
    length = decays.shape[1]
    below_diag = (jnp.arange(length)[:, None] >= jnp.arange(length)[None, :])[None]
    spread = running[:, :, None] - running[:, None, :]
    within = jnp.where(below_diag, jnp.exp(jnp.where(below_diag, spread, 0.0)), 0.0)
    return (jnp.exp(finish), jnp.exp(finish[:, None] - running), jnp.exp(running), within)


def chain_join(earlier, later):
    return (earlier[0] * later[0], later[0][:, None, None] * earlier[1] + later[1])


def sparse_grads(queries, grads_out, key_rows, value_rows, allowed):
    score_scale = queries.shape[-1] ** (-0.5)
    scores = (
        jnp.einsum("bqhd,bkhd->bhqk", queries, key_rows, preferred_element_type=jnp.float32)
        * score_scale
    )
    key_mask = allowed[:, None]
    scores = jnp.where(key_mask, scores, -1e30)
    row_max = jnp.max(scores, axis=-1, keepdims=True)
    weights = jnp.where(key_mask, jnp.exp(scores - row_max), 0.0)
    softmax_probs = weights / jnp.sum(weights, axis=-1, keepdims=True)
    rounded = softmax_probs.astype(jnp.bfloat16)
    outputs = jnp.einsum("bhqk,bkhd->bqhd", rounded, value_rows, preferred_element_type=jnp.float32)
    row_delta = jnp.sum(grads_out.astype(jnp.float32) * outputs, axis=-1)
    grad_probs = jnp.einsum(
        "bqhd,bkhd->bhqk", grads_out, value_rows, preferred_element_type=jnp.float32
    )
    grad_scores = (
        softmax_probs * (grad_probs - jnp.transpose(row_delta, (0, 2, 1))[..., None])
    ).astype(jnp.bfloat16)
    query_gradient = (
        jnp.einsum("bhqk,bkhd->bqhd", grad_scores, key_rows, preferred_element_type=jnp.float32)
        * score_scale
    )
    key_gradient = (
        jnp.einsum("bhqk,bqhd->bkhd", grad_scores, queries, preferred_element_type=jnp.float32)
        * score_scale
    )
    value_gradient = jnp.einsum(
        "bhqk,bqhd->bkhd", rounded, grads_out, preferred_element_type=jnp.float32
    )
    return (query_gradient, key_gradient, value_gradient)


def local(
    lin_q,
    lin_k,
    lin_v,
    lin_decay,
    norm_gain,
    soft_q,
    soft_k,
    soft_v,
    out_grad,
    block_lists,
    block_counts,
):
    tok_rows, heads_here, head_width = lin_q.shape
    blocks_here = tok_rows // BLK
    span_count = lax.axis_size("ctx")
    own_span = lax.axis_index("ctx")
    total_width = heads_here * lax.axis_size("head") * head_width
    complete_query = lin_q.astype(jnp.float32)
    complete_key = lin_k.astype(jnp.float32)
    complete_value = lin_v.astype(jnp.float32)
    carry_decay, trailing_decay, leading_decay, within = decay_tables(lin_decay)
    state_here = jnp.einsum(
        "boz,bor->ozr",
        complete_key * trailing_decay.T[:, :, None],
        complete_value,
        precision=exact_precision,
    )
    identity = (jnp.ones_like(carry_decay), jnp.zeros_like(state_here))
    incoming_state = carried_in((carry_decay, state_here), "ctx", chain_join, identity, False)[1]
    pair_weights = (
        jnp.einsum("thk,shk->hts", lin_q, lin_k, preferred_element_type=jnp.float32) * within
    )
    layer_out = jnp.einsum("hts,shv->thv", pair_weights, complete_value, precision=exact_precision)
    layer_out = layer_out + leading_decay.T[:, :, None] * jnp.einsum(
        "wfg,fgl->wfl", complete_query, incoming_state, precision=exact_precision
    )
    squares = lax.psum(jnp.sum(layer_out * layer_out, axis=(1, 2)), "head")
    root_mean = jnp.sqrt(squares / total_width + epsilon)
    norm_scale = norm_gain[None]
    all_lists, all_counts = (
        lax.all_gather(block_lists, "ctx", axis=0, tiled=True),
        lax.all_gather(block_counts, "ctx", axis=0, tiled=True),
    )
    entries = blocks_here * NSEL
    every_live = (
        jnp.arange(NSEL)[None, None, :] < all_counts.reshape(span_count, blocks_here)[:, :, None]
    ).reshape(span_count, entries)
    owner_hits = every_live & (all_lists // blocks_here == own_span)
    wanted_here = jnp.max(jnp.where(owner_hits, all_lists % blocks_here, -1), axis=1)
    my_live = jnp.arange(NSEL)[None, :] < block_counts[:, None]
    flat_owner = (block_lists // blocks_here).reshape(entries)
    flat_live = my_live.reshape(entries)
    key_blocks = soft_k.reshape(blocks_here, BLK, heads_here, head_width)
    value_blocks = soft_v.reshape(blocks_here, BLK, heads_here, head_width)
    owners = jnp.arange(span_count)
    matches = flat_live[None, :] & (flat_owner[None, :] == owners[:, None])
    wanted_ids = jnp.max(jnp.where(matches, block_lists.reshape(entries)[None, :], -1), axis=1)
    empty_slot = jnp.zeros((span_count, BLK, heads_here, head_width), jnp.bfloat16)
    shard_piece = (
        lax.all_gather(soft_k, "ctx", axis=0, tiled=True),
        lax.all_gather(soft_v, "ctx", axis=0, tiled=True),
    )
    row_count = shard_piece[0].shape[0]
    token_index = wanted_ids[:, None] * BLK + jnp.arange(BLK)[None, :]
    usable = ((wanted_ids[:, None] >= 0) & (token_index >= 0) & (token_index < row_count))[
        :, :, None, None
    ]
    safe_index = jnp.clip(token_index, 0, row_count - 1)
    new_keys = jnp.where(usable, shard_piece[0][safe_index], empty_slot)
    new_values = jnp.where(usable, shard_piece[1][safe_index], empty_slot)
    listed_keys = jnp.take(new_keys, flat_owner, axis=0).reshape(
        blocks_here, NSEL * BLK, heads_here, head_width
    )
    listed_values = jnp.take(new_values, flat_owner, axis=0).reshape(
        blocks_here, NSEL * BLK, heads_here, head_width
    )
    key_rows = jnp.concatenate([key_blocks, listed_keys], axis=1)
    value_rows = jnp.concatenate([value_blocks, listed_values], axis=1)
    causal = jnp.arange(BLK)[:, None] >= jnp.arange(BLK)[None, :]
    remote_mask = jnp.broadcast_to(
        jnp.repeat(my_live, BLK, axis=1)[:, None, :], (blocks_here, BLK, NSEL * BLK)
    )
    allowed = jnp.concatenate(
        [jnp.broadcast_to(causal, (blocks_here, BLK, BLK)), remote_mask], axis=2
    )
    query_blocks = soft_q.reshape(blocks_here, BLK, heads_here, head_width)
    grad_blocks = out_grad.reshape(blocks_here, BLK, heads_here, head_width)
    query_gradient, key_gradient, value_gradient = sparse_grads(
        query_blocks, grad_blocks, key_rows, value_rows, allowed
    )
    soft_dq = query_gradient.reshape(tok_rows, heads_here, head_width).astype(jnp.bfloat16)
    routing = (
        flat_live[None, :] & (flat_owner[None, :] == jnp.arange(span_count)[:, None])
    ).astype(jnp.float32)
    remote_key = key_gradient[:, BLK:].reshape(entries, BLK, heads_here, head_width)
    remote_value = value_gradient[:, BLK:].reshape(entries, BLK, heads_here, head_width)
    part_key = jnp.einsum("oe,exhd->oxhd", routing, remote_key, precision=exact_precision).astype(
        jnp.bfloat16
    )
    part_value = jnp.einsum(
        "oe,exhd->oxhd", routing, remote_value, precision=exact_precision
    ).astype(jnp.bfloat16)
    back_key, back_value = (
        lax.all_to_all(part_key, "ctx", split_axis=0, concat_axis=0, tiled=True),
        lax.all_to_all(part_value, "ctx", split_axis=0, concat_axis=0, tiled=True),
    )
    placing = (wanted_here[:, None] == jnp.arange(blocks_here)[None, :]).astype(jnp.float32)
    added_key = jnp.einsum(
        "rb,rxhd->bxhd", placing, back_key.astype(jnp.float32), precision=exact_precision
    ).reshape(tok_rows, heads_here, head_width)
    added_value = jnp.einsum(
        "rb,rxhd->bxhd", placing, back_value.astype(jnp.float32), precision=exact_precision
    ).reshape(tok_rows, heads_here, head_width)
    soft_dk = (key_gradient[:, :BLK].reshape(tok_rows, heads_here, head_width) + added_key).astype(
        jnp.bfloat16
    )
    value_total = value_gradient[:, :BLK].reshape(tok_rows, heads_here, head_width) + added_value
    soft_dv = value_total.astype(jnp.bfloat16)
    cotangent = out_grad.astype(jnp.float32) + value_total
    inner_total = lax.psum(jnp.sum(norm_scale * cotangent * layer_out, axis=(1, 2)), "head")
    linear_cotangent = (
        norm_scale * cotangent / root_mean[:, None, None]
        - layer_out * (inner_total / (total_width * root_mean**3))[:, None, None]
    )
    reverse_state = carried_in(
        (
            carry_decay,
            jnp.einsum(
                "boz,bor->ozr",
                complete_query * leading_decay.T[:, :, None],
                linear_cotangent,
                precision=exact_precision,
            ),
        ),
        "ctx",
        chain_join,
        identity,
        True,
    )[1]
    grad_pair = (
        jnp.einsum("thv,shv->hts", linear_cotangent, complete_value, precision=exact_precision)
        * within
    )
    lin_dq = jnp.einsum("hts,shk->thk", grad_pair, complete_key, precision=exact_precision)
    lin_dq = lin_dq + leading_decay.T[:, :, None] * jnp.einsum(
        "fqs,qrs->fqr", linear_cotangent, incoming_state, precision=exact_precision
    )
    lin_dk = jnp.einsum("hts,thk->shk", grad_pair, complete_query, precision=exact_precision)
    lin_dk = lin_dk + trailing_decay.T[:, :, None] * jnp.einsum(
        "fut,ujt->fuj", complete_value, reverse_state, precision=exact_precision
    )
    lin_dv = jnp.einsum("hts,thv->shv", pair_weights, linear_cotangent, precision=exact_precision)
    lin_dv = lin_dv + trailing_decay.T[:, :, None] * jnp.einsum(
        "zpu,pux->zpx", complete_key, reverse_state, precision=exact_precision
    )
    return (
        lin_dq.astype(jnp.bfloat16),
        lin_dk.astype(jnp.bfloat16),
        lin_dv.astype(jnp.bfloat16),
        soft_dq,
        soft_dk,
        soft_dv,
    )


def solution(mesh):
    in_specs = (
        P("ctx", "head", None),
        P("ctx", "head", None),
        P("ctx", "head", None),
        P("head", "ctx"),
        P("head", None),
        P("ctx", "head", None),
        P("ctx", "head", None),
        P("ctx", "head", None),
        P("ctx", "head", None),
        P("ctx", None),
        P("ctx"),
    )
    out_specs = (
        P("ctx", "head", None),
        P("ctx", "head", None),
        P("ctx", "head", None),
        P("ctx", "head", None),
        P("ctx", "head", None),
        P("ctx", "head", None),
    )
    return jax.shard_map(local, mesh=mesh, in_specs=in_specs, out_specs=out_specs, check_vma=False)
```

profile of v0, /device:TPU:32, one launch (start us, length us, event | category | flops | bytes accessed | tf_op | source)
XLA Modules:
  0.0 770.6 jit_solution(8444766852220716513)
XLA Ops:
  11.1 2.1 fusion.51
  17.2 1.3 add_bitcast_fusion
  18.5 76.2 %all-gather.11.cloned.1.call-done = bf16[4096,4,128]{2,1,0:T(4,128)(2,1)} async-done(((bf16[128,4,128]{2,1,0:T(4,128)(2,1)}), bf16[4096,4,128]{2,1,0:T(4,128)(2,1)}) %all-gather.11.cloned.1.call-update) | async-done | bytes 4194320 | tf_op jit(solution)/shard_map/all_gather | solution.py:139
  94.7 30.5 %gather_fusion.1 = bf16[4096,4,128]{2,1,0:T(4,128)(2,1)} fusion(bf16[4096,4,128]{2,1,0:T(4,128)(2,1)} %all-gather.11.cloned.1.call-done, s32[4096]{0:T(1024)S(1)} %fusion.73), kind=kCustom, calls=%fused_computation.3 | custom fusion | bytes 8404992 | tf_op jit(solution)/shard_map/gather | solution.py:148
  125.2 50.7 %all-gather.9.cloned.1.call-done = bf16[4096,4,128]{2,1,0:T(4,128)(2,1)} async-done(((bf16[128,4,128]{2,1,0:T(4,128)(2,1)}), bf16[4096,4,128]{2,1,0:T(4,128)(2,1)}) %all-gather.9.cloned.1.call-update) | async-done | bytes 4194320 | tf_op jit(solution)/shard_map/all_gather | solution.py:138
  175.9 30.5 %gather_fusion = bf16[4096,4,128]{2,1,0:T(4,128)(2,1)} fusion(bf16[4096,4,128]{2,1,0:T(4,128)(2,1)} %all-gather.9.cloned.1.call-done, s32[4096]{0:T(1024)S(1)} %fusion.73), kind=kCustom, calls=%fused_computation.2 | custom fusion | bytes 8404992 | tf_op jit(solution)/shard_map/gather | solution.py:147
  206.4 6.7 copy_select_fusion
  213.0 3.2 gather_fusion.3
  216.2 4.4 gather_fusion.2
  220.6 3.4 broadcast_select_fusion
  224.2 3.9 fusion.102
  228.1 2.7 fusion.24
  231.8 1.7 copy-done.1
  233.5 7.4 fusion.18
  241.0 4.2 copy.213
  245.2 6.6 all-to-all-start
  253.3 170.3 %all-reduce.1 = f32[128]{0:T(128)S(1)} all-reduce(f32[128]{0:T(128)S(1)} %dynamic-update-slice.1), channel_id=2, replica_groups=mesh['ctx'=32,'head'=8] {'ctx'}, use_global_device_ids=true, to_apply=%add.1 | all-reduce | flops 128 | bytes 1024
  423.8 37.6 %all-gather.3 = s32[32,1,16]{2,1,0:T(1,128)S(1)} all-gather(s32[1,1,16]{2,1,0:T(1,128)S(1)} %bitcast.233), channel_id=1, replica_groups=mesh['ctx'=32,'head'=8] {'ctx'}, dimensions={0}, use_global_device_ids=true | all-gather | bytes 2112 | tf_op jit(solution)/shard_map/all_gather | solution.py:119
  462.2 18.1 %all-reduce = s32[32]{0:T(128)S(1)} all-reduce(s32[32]{0:T(128)S(1)} %dynamic-update-slice), channel_id=1, replica_groups=mesh['ctx'=32,'head'=8] {'ctx'}, use_global_device_ids=true, to_apply=%add | all-reduce | flops 32 | bytes 256
  482.1 1.1 while.26
  482.1 1.1 bitcast_add_fusion.4
  483.8 4.6 fusion.12
  488.4 2.0 multiply_reduce_fusion.1
  490.5 12.6 %all-reduce.2 = (f32[128]{0:T(128)S(1)}, f32[128]{0:T(128)S(1)}) all-reduce(f32[128]{0:T(128)S(1)} %get-tuple-element.168, f32[128]{0:T(128)S(1)} %get-tuple-element.167), channel_id=1, replica_groups=mesh['ctx'=32,'head'=8] {'head'}, use_global_device_ids=true, to_apply=%region_10.12 | all-reduce | flops 256 | bytes 2048 | tf_op jit(solution)/shard_map/psum | solution.py:198
  503.1 1.2 multiply_subtract_fusion
  504.4 2.1 fusion.48
  507.4 1.8 copy.241
  509.2 1.9 fusion.43
  511.1 3.1 fusion.9
  515.2 1.8 copy-done.2
  517.0 7.2 fusion.21
  524.3 4.1 copy.250
  528.4 38.5 %all-to-all-start.1 = ((bf16[32,128,4,128]{3,2,1,0:T(4,128)(2,1)}), bf16[32,128,4,128]{3,2,1,0:T(4,128)(2,1)}, u32[]{:S(2)}, u32[]{:S(2)}) async-start(bf16[32,128,4,128]{3,2,1,0:T(4,128)(2,1)} %copy.250), calls=%async_computation.1 | async-start | bytes 8388608 | tf_op jit(solution)/shard_map/all_to_all | solution.py:182
  566.9 2.5 fusion.42
  570.2 128.2 %all-to-all-done.1 = bf16[32,128,4,128]{3,2,1,0:T(4,128)(2,1)} async-done(((bf16[32,128,4,128]{3,2,1,0:T(4,128)(2,1)}), bf16[32,128,4,128]{3,2,1,0:T(4,128)(2,1)}, u32[]{:S(2)}, u32[]{:S(2)}) %all-to-all-start.1) | async-done | bytes 4194336 | tf_op jit(solution)/shard_map/all_to_all | solution.py:182
  698.3 4.6 fusion.10
  708.6 53.2 %while.27 = (s32[]{:T(128)}, f32[4,128,128]{2,1,0:T(8,128)S(1)}, s32[]{:T(128)}, f32[32,4]{1,0:T(8,128)}, f32[32,4,128,128]{3,2,1,0:T(8,128)}, /*index=5*/s32[]{:T(128)}, s32[]{:T(128)}, s32[]{:T(128)}, s32[]{:T(128)}) while((s32[]{:T(128)}, f32[4,128,128]{2,1,0:T(8,128)S(1)}, s32[]{:T(128)}, f32[32,4]{1,0:T(8,128)}, ...), condition=%wide.region_12.14_spmd, body=%wide.region_11.13_spmd.sunk | while | flops 131078 | bytes 786635 | solution.py:27
  709.3 1.1 bitcast_add_fusion.5
  711.1 1.1 bitcast_add_fusion.5
  712.9 1.1 bitcast_add_fusion.5
  714.6 1.1 bitcast_add_fusion.5
  716.4 1.1 bitcast_add_fusion.5
  718.2 1.1 bitcast_add_fusion.5
  720.0 1.1 bitcast_add_fusion.5
  721.7 1.1 bitcast_add_fusion.5
  723.5 1.1 bitcast_add_fusion.5
  727.1 1.1 bitcast_add_fusion.5
  728.8 1.1 bitcast_add_fusion.5
  (165 shorter events, 63.9 us)
Async XLA Ops:
  7.2 217.0 %copy-start = (bf16[128,4,128]{2,1,0:T(4,128)(2,1)S(1)}, bf16[128,4,128]{2,1,0:T(4,128)(2,1)}, u32[]{:S(2)}) copy-start(bf16[128,4,128]{2,1,0:T(4,128)(2,1)} %param.22) | copy-start | bytes 393220
  7.2 87.5 %all-gather.11.cloned.1.call-start = ((), (), s32[]{:S(2)}) async-start(), calls=%async_computation.3 | async-start | bytes 4325376 | tf_op jit(solution)/shard_map/all_gather | solution.py:139
  7.9 168.0 %all-gather.9.cloned.1.call-start = ((), (), s32[]{:S(2)}) async-start(), calls=%async_computation.2 | async-start | bytes 4325376 | tf_op jit(solution)/shard_map/all_gather | solution.py:138
  8.7 473.4 %all-gather.13.cloned.1.call-start = ((), (), s32[]{:S(2)}) async-start(), calls=%async_computation.4 | async-start | bytes 8650752 | tf_op jit(solution)/shard_map/all_gather | solution.py:18
  9.7 471.1 %copy-start.15 = (f32[4,128]{1,0:T(4,128)}, f32[4,128]{1,0:T(4,128)S(1)}, u32[]{:S(2)}) copy-start(f32[4,128]{1,0:T(4,128)S(1)} %reduce_window_sum.11) | copy-start | bytes 6148
  10.5 0.6 copy-start.17
  14.2 210.0 %copy-start.13 = (bf16[128,4,128]{2,0,1:T(8,128)(2,1)}, bf16[128,4,128]{2,0,1:T(8,128)(2,1)S(1)}, u32[]{:S(2)}) copy-start(bf16[128,4,128]{2,0,1:T(8,128)(2,1)S(1)} %copy.353) | copy-start | bytes 393220
  14.8 218.7 %copy-start.23 = (pred[16]{0:T(512)(128)(4,1)}, pred[16]{0:T(512)(128)(4,1)S(1)}, u32[]{:S(2)}) copy-start(pred[16]{0:T(512)(128)(4,1)S(1)} %iota_compare_fusion.4) | copy-start | bytes 52
  224.2 3.9 copy-start.3
  228.1 3.4 copy-start.25
  228.1 2.7 copy-start.7
  231.5 2.0 copy-start.1
  231.5 2.0 copy-start.21
  245.1 6.7 copy-start.27
  245.1 235.7 %copy-start.5 = (bf16[128,4,128]{2,1,0:T(4,128)(2,1)S(1)}, bf16[128,4,128]{2,1,0:T(4,128)(2,1)}, u32[]{:S(2)}) copy-start(bf16[128,4,128]{2,1,0:T(4,128)(2,1)} %param.17) | copy-start | bytes 393220
  245.2 235.7 %copy-start.6 = (bf16[128,4,128]{2,1,0:T(4,128)(2,1)S(1)}, bf16[128,4,128]{2,1,0:T(4,128)(2,1)}, u32[]{:S(2)}) copy-start(bf16[128,4,128]{2,1,0:T(4,128)(2,1)} %param.18) | copy-start | bytes 393220
  245.2 235.9 %copy-start.4 = (bf16[128,4,128]{2,1,0:T(4,128)(2,1)S(1)}, bf16[128,4,128]{2,1,0:T(4,128)(2,1)}, u32[]{:S(2)}) copy-start(bf16[128,4,128]{2,1,0:T(4,128)(2,1)} %param.19) | copy-start | bytes 393220
  245.2 238.6 %all-to-all-start = ((bf16[32,128,4,128]{3,2,1,0:T(4,128)(2,1)}), bf16[32,128,4,128]{3,2,1,0:T(4,128)(2,1)}, u32[]{:S(2)}, u32[]{:S(2)}) async-start(bf16[32,128,4,128]{3,2,1,0:T(4,128)(2,1)} %copy.213), calls=%async_computation | async-start | bytes 8388608 | tf_op jit(solution)/shard_map/all_to_all | solution.py:183
  251.8 456.8 %all-gather.15.cloned.1.call-start = ((), (), s32[]{:S(2)}) async-start(), calls=%async_computation.5 | async-start | bytes 8650752 | tf_op jit(solution)/shard_map/all_gather | solution.py:18
  481.1 2.1 copy-start.9
  483.2 0.6 copy-start.20
  483.8 4.7 copy-start.11
  509.2 1.9 copy-start.8
  509.2 1.9 copy-start.26
  514.9 2.1 copy-start.2
  514.9 2.1 copy-start.22
  514.9 2.1 copy-start.24
  528.4 38.5 %copy-start.14 = (bf16[128,4,128]{2,0,1:T(8,128)(2,1)S(1)}, bf16[128,4,128]{2,0,1:T(8,128)(2,1)}, u32[]{:S(2)}) copy-start(bf16[128,4,128]{2,0,1:T(8,128)(2,1)} %copy-done.13) | copy-start | bytes 393220
  528.4 170.0 %all-to-all-start.1 = ((bf16[32,128,4,128]{3,2,1,0:T(4,128)(2,1)}), bf16[32,128,4,128]{3,2,1,0:T(4,128)(2,1)}, u32[]{:S(2)}, u32[]{:S(2)}) async-start(bf16[32,128,4,128]{3,2,1,0:T(4,128)(2,1)} %copy.250), calls=%async_computation.1 | async-start | bytes 8388608 | tf_op jit(solution)/shard_map/all_to_all | solution.py:182
  569.4 135.3 %copy-start.12 = (bf16[128,4,128]{2,0,1:T(8,128)(2,1)S(1)}, bf16[128,4,128]{2,0,1:T(8,128)(2,1)}, u32[]{:S(2)}) copy-start(bf16[128,4,128]{2,0,1:T(8,128)(2,1)} %get-tuple-element.193) | copy-start | bytes 393220
  569.4 136.1 %copy-start.16 = (f32[4,128]{1,0:T(4,128)S(1)}, f32[4,128]{1,0:T(4,128)}, u32[]{:S(2)}) copy-start(f32[4,128]{1,0:T(4,128)} %copy-done.15) | copy-start | bytes 6148
  569.4 136.7 %copy-start.19 = (f32[128,4]{0,1:T(4,128)S(1)}, f32[128,4]{0,1:T(4,128)}, u32[]{:S(2)}) copy-start(f32[128,4]{0,1:T(4,128)} %get-tuple-element.196) | copy-start | bytes 6148
  570.2 137.8 %copy-start.10 = (f32[4,128,128]{2,1,0:T(8,128)S(1)}, f32[4,128,128]{2,1,0:T(8,128)}, u32[]{:S(2)}) copy-start(f32[4,128,128]{2,1,0:T(8,128)} %copy-done.9) | copy-start | bytes 786436
  705.5 56.4 %copy-start.18 = (f32[128,4]{0,1:T(4,128)S(1)}, f32[128,4]{0,1:T(4,128)}, u32[]{:S(2)}) copy-start(f32[128,4]{0,1:T(4,128)} %copy-done.17) | copy-start | bytes 6148
Sparse Core Ops, SparseCore 0:
  10.6 84.0 all-gather.10
  97.3 78.5 all-gather.8
  178.5 149.4 all-gather.12
  506.6 193.3 all-gather.14
where the time goes:
time: 773 us; the launch traced here: 771 us
  waiting for transfers between devices  256 us (33%)
  blocking collectives  239 us (31%)
  local copies, waits for them, and re-layouts  114 us (15%)
  other arithmetic  53.3 us (7%)
  matrix products  47 us (6%)
  starting transfers between devices  45.2 us (6%)
  between operations  15.6 us (2%)
    unnamed x2, blocking collectives  188 us
    all_to_all x1, waiting for transfers between devices, local(): lax.all_to_all(part_key, 'ctx', split_axis=0, concat_axis=0, tiled=True)  128 us
    all_gather x1, waiting for transfers between devices, local(): lax.all_gather(soft_v, 'ctx', axis=0, tiled=True)  76.2 us
    all_gather x1, waiting for transfers between devices, local(): lax.all_gather(soft_k, 'ctx', axis=0, tiled=True)  50.7 us
    all_to_all x1, starting transfers between devices, local(): lax.all_to_all(part_key, 'ctx', split_axis=0, concat_axis=0, tiled=True)  38.5 us
    all_gather x1, blocking collectives, local(): lax.all_gather(block_lists, 'ctx', axis=0, tiled=True)  37.6 us
    add x31, other arithmetic, chain_join(): later[0][:, None, None] * earlier[1] + later[1]  32.7 us
    gather x1, local copies, waits for them, and re-layouts, local(): new_keys = jnp.where(usable, shard_piece[0][safe_index], empty_slot)  30.5 us
  transfers between devices with their start and end apart: 6, of which 3 were waited for; matrix products, arithmetic and copies ran while one was open for 19% of the time, Pallas kernels for 0%

commit v1 on v0

v1 whole, which is shorter than its diff:
```python
import functools

import jax
import jax.numpy as jnp
from jax import lax
from jax.experimental import pallas as pl
from jax.experimental.pallas import tpu as pltpu
from jax.sharding import PartitionSpec as P

NY = 4
HL = 4
B = 128
NSEL = 16
EPS = 1e-05
SCALE = 128 ** (-0.5)
NEG = -1e30
BIG = 1e30
F32 = jnp.float32
BF16 = jnp.bfloat16
MESH = pl.DeviceIdType.MESH
HIGH = lax.Precision.HIGHEST


def mm(a, b):
    return lax.dot_general(a, b, (((1,), (0,)), ((), ())), preferred_element_type=F32)


def mm_t(a, b):
    return lax.dot_general(a, b, (((1,), (1,)), ((), ())), preferred_element_type=F32)


def t_mm(a, b):
    return lax.dot_general(a, b, (((0,), (0,)), ((), ())), preferred_element_type=F32)


def iota(dim):
    return lax.broadcasted_iota(jnp.int32, (B, B), dim)


def col_of(row):
    return jnp.transpose(jnp.broadcast_to(row, (B, B)))


def row_of(col):
    return jnp.transpose(jnp.broadcast_to(col, (B, B)))[0:1]


def running_of(decay):
    upper = (iota(0) <= iota(1)).astype(F32)
    return lax.dot_general(
        decay, upper, (((1,), (0,)), ((), ())), precision=HIGH, preferred_element_type=F32
    )


def within_of(row, col):
    keep = iota(0) >= iota(1)
    return jnp.where(keep, jnp.exp(jnp.where(keep, col - row, 0.0)), 0.0)


def slot_of(r, y):
    return jnp.where(lax.rem(y + 3, NY) == r, 0, jnp.where(lax.rem(y + 1, NY) == r, 1, 2))


def place(nz):
    own = lax.axis_index("ctx")
    return own // nz, lax.rem(own, nz)


def start_remote(src, dst, send, recv, ctx, head):
    pltpu.make_async_remote_copy(
        src_ref=src, dst_ref=dst, send_sem=send, recv_sem=recv, device_id=(ctx, head), device_id_type=MESH
    ).start()


def wait_recv(ref, recv, ctx, head):
    pltpu.make_async_remote_copy(
        src_ref=ref, dst_ref=ref, send_sem=recv, recv_sem=recv, device_id=(ctx, head), device_id_type=MESH
    ).wait_recv()


def wait_send(ref, send, ctx, head):
    pltpu.make_async_remote_copy(
        src_ref=ref, dst_ref=ref, send_sem=send, recv_sem=send, device_id=(ctx, head), device_id_type=MESH
    ).wait_send()


def prep_kernel(lq, lk, lv, sq, sk, sv, og, dec, own, lin, state, fin, tmp):
    def heads(ref, store):
        tmp[...] = ref[...].astype(F32)
        for h in range(HL):
            store(h, tmp[pl.ds(h, B, stride=HL), :].astype(BF16))

    def into(dst, a):
        def store(h, value):
            dst[h, a] = value

        return store

    heads(sk, into(own, 0))
    heads(sv, into(own, 1))
    heads(sq, into(own, 2))
    heads(og, into(own, 3))
    heads(lq, into(lin, 0))
    heads(lk, into(lin, 1))
    heads(lv, into(lin, 2))
    run = running_of(dec[...])
    finish = run[:, B - 1 : B]
    fin[...] = jnp.concatenate([jnp.broadcast_to(finish, (HL, B))] * 2, axis=0)
    trailing = jnp.exp(finish - run)
    for h in range(HL):
        k = lin[h, 1].astype(F32) * col_of(trailing[h : h + 1])
        state[pl.ds(h * B, B), :] = t_mm(k.astype(BF16), lin[h, 2]).astype(BF16)


def prep(arrays, decay):
    full = pl.BlockSpec(memory_space=pltpu.VMEM)
    return pl.pallas_call(
        prep_kernel,
        out_shape=(
            jax.ShapeDtypeStruct((HL, 4, B, B), BF16),
            jax.ShapeDtypeStruct((HL, 3, B, B), BF16),
            jax.ShapeDtypeStruct((HL * B, B), BF16),
            jax.ShapeDtypeStruct((2 * HL, B), F32),
        ),
        in_specs=[full] * 8,
        out_specs=(full,) * 4,
        scratch_shapes=[pltpu.VMEM((HL * B, B), F32)],
    )(*arrays, decay)


def scan_scratch(nz):
    rs = HL * B // nz
    return [
        pltpu.VMEM((nz, rs, B), BF16),
        pltpu.VMEM((nz, rs, B), F32),
        pltpu.VMEM((NY, rs, B), F32),
        pltpu.VMEM((rs, B), F32),
        pltpu.VMEM((nz, rs, B), BF16),
        pltpu.SemaphoreType.DMA((6, nz)),
        pltpu.SemaphoreType.DMA((2,)),
    ]


def scan_start(nz, head, local, bufs):
    zbuf, sems, lsem = bufs[0], bufs[5], bufs[6]
    rs = HL * B // nz
    y, z = place(nz)
    for d in range(1, nz):
        zz = lax.rem(z + d, nz)
        start_remote(
            local.at[pl.ds(zz * rs, rs)], zbuf.at[z], sems.at[0, zz], sems.at[1, z], y * nz + zz, head
        )
    pltpu.make_async_copy(local.at[pl.ds(z * rs, rs)], zbuf.at[z], lsem.at[0]).start()


def scan_rows(nz, head, local, fin, bufs, reverse):
    zbuf, ebuf, tbuf, tsrc, _, sems, lsem = bufs
    rs = HL * B // nz
    y, z = place(nz)
    own = y * nz + z
    hz = z * rs // B
    pltpu.make_async_copy(local.at[pl.ds(z * rs, rs)], zbuf.at[z], lsem.at[0]).wait()
    for d in range(1, nz):
        zz = lax.rem(z + d, nz)
        wait_recv(zbuf.at[zz], sems.at[1, zz], own, head)

    total = jnp.zeros((rs, B), F32)
    for lap in range(nz):
        m = nz - 1 - lap if reverse else lap
        ebuf[m] = total
        total = total * jnp.exp(fin[y, m, pl.ds(hz, 1), :]) + zbuf[m].astype(F32)
    tsrc[...] = total
    for d in range(1, NY):
        yy = lax.rem(y + d, NY)
        start_remote(tsrc, tbuf.at[y], sems.at[2, yy], sems.at[3, y], yy * nz + z, head)
    for d in range(1, nz):
        zz = lax.rem(z + d, nz)
        wait_send(zbuf.at[0], sems.at[0, zz], own, head)


def scan_spread(nz, head, fin, out, bufs, reverse):
    _, ebuf, tbuf, tsrc, sbuf, sems, lsem = bufs
    rs = HL * B // nz
    y, z = place(nz)
    own = y * nz + z
    hz = z * rs // B
    for d in range(1, NY):
        yy = lax.rem(y + d, NY)
        wait_recv(tbuf.at[yy], sems.at[3, yy], own, head)
        wait_send(tsrc, sems.at[2, yy], own, head)
    carry = jnp.zeros((rs, B), F32)
    for lap in range(NY):
        r = NY - 1 - lap if reverse else lap
        use = (r > y) if reverse else (r < y)
        span = jnp.zeros((1, B), F32)
        for m in range(nz):
            span = span + fin[r, m, pl.ds(hz, 1), :]
        carry = jnp.where(use, carry * jnp.exp(span) + tbuf[r], carry)
    for lap in range(nz):
        m = nz - 1 - lap if reverse else lap
        sbuf[m] = (ebuf[m] + carry).astype(BF16)
        carry = carry * jnp.exp(fin[y, m, pl.ds(hz, 1), :])
    for d in range(1, nz):
        zz = lax.rem(z + d, nz)
        start_remote(
            sbuf.at[zz], out.at[pl.ds(z * rs, rs)], sems.at[4, zz], sems.at[5, z], y * nz + zz, head
        )
    pltpu.make_async_copy(sbuf.at[z], out.at[pl.ds(z * rs, rs)], lsem.at[1]).start()


def scan_finish(nz, head, out, bufs):
    sbuf, sems, lsem = bufs[4], bufs[5], bufs[6]
    rs = HL * B // nz
    y, z = place(nz)
    own = y * nz + z
    for d in range(1, nz):
        zz = lax.rem(z + d, nz)
        wait_recv(out.at[pl.ds(zz * rs, rs)], sems.at[5, zz], own, head)
        wait_send(sbuf.at[zz], sems.at[4, zz], own, head)
    pltpu.make_async_copy(sbuf.at[z], out.at[pl.ds(z * rs, rs)], lsem.at[1]).wait()


def small_start(nz, head, src, dst, sems):
    y, z = place(nz)
    for d in range(1, nz):
        zz = lax.rem(z + d, nz)
        start_remote(src, dst.at[y, z], sems.at[0, zz], sems.at[1, z], y * nz + zz, head)
    pltpu.make_async_copy(src, dst.at[y, z], sems.at[2, 0]).start()


def small_rows(nz, head, src, dst, sems):
    y, z = place(nz)
    own = y * nz + z
    for d in range(1, nz):
        zz = lax.rem(z + d, nz)
        wait_recv(dst.at[y, zz], sems.at[1, zz], own, head)
    pltpu.make_async_copy(src, dst.at[y, z], sems.at[2, 0]).wait()
    for d in range(1, NY):
        yy = lax.rem(y + d, NY)
        start_remote(dst.at[y], dst.at[y], sems.at[3, yy], sems.at[4, y], yy * nz + z, head)


def small_finish(nz, head, src, dst, sems):
    y, z = place(nz)
    own = y * nz + z
    for d in range(1, NY):
        yy = lax.rem(y + d, NY)
        wait_recv(dst.at[yy], sems.at[4, yy], own, head)


def small_drain(nz, head, src, dst, sems):
    y, z = place(nz)
    own = y * nz + z
    for d in range(1, nz):
        zz = lax.rem(z + d, nz)
        wait_send(src, sems.at[0, zz], own, head)
    for d in range(1, NY):
        yy = lax.rem(y + d, NY)
        wait_send(dst.at[y], sems.at[3, yy], own, head)


def greet(nz, head, nh):
    y, z = place(nz)
    barrier = pltpu.get_barrier_semaphore()
    for d in range(1, nz):
        pl.semaphore_signal(
            barrier, inc=1, device_id=(y * nz + lax.rem(z + d, nz), head), device_id_type=MESH
        )
    for d in range(1, NY):
        pl.semaphore_signal(
            barrier, inc=1, device_id=(lax.rem(y + d, NY) * nz + z, head), device_id_type=MESH
        )
    for d in range(1, nh):
        pl.semaphore_signal(
            barrier, inc=1, device_id=(y * nz + z, lax.rem(head + d, nh)), device_id_type=MESH
        )
    pl.semaphore_wait(barrier, nz - 1 + NY - 1 + nh - 1)


def exchange_kernel(
    nz, own, state, fin_own, pairs, state_in, fin, ring_s, ring_r, bun_s, bun_r, up_s, dn_s, col_r, rel_s, fsem, *bufs
):
    head = lax.axis_index("head")
    y, z = place(nz)
    me = y * nz + z
    right, left = y * nz + lax.rem(z + 1, nz), y * nz + lax.rem(z + nz - 1, nz)
    above, below = lax.rem(y + 1, NY) * nz + z, lax.rem(y + NY - 1, NY) * nz + z
    part_up = jnp.where(y < NY - 1, 0, 1)
    part_dn = jnp.where(y > 0, 1, 0)
    inner = (y == 1) | (y == 2)
    greet(nz, head, 1)
    small_start(nz, head, fin_own, fin, fsem)
    scan_start(nz, head, state, bufs)

    def ring_own(h, to):
        start_remote(own.at[h], pairs.at[z, h, pl.ds(3, 2)], ring_s.at[z, h], ring_r.at[z, h], to, head)

    def ring_on(zz, h, to):
        ref = pairs.at[zz, h, pl.ds(3, 2)]
        start_remote(ref, ref, ring_s.at[zz, h], ring_r.at[zz, h], to, head)

    def ring_wait(zz, h):
        wait_recv(pairs.at[zz, h, pl.ds(3, 2)], ring_r.at[zz, h], me, head)

    def bundle_on(zz, h, to):
        ref = pairs.at[zz, h, pl.ds(0, 3)]
        start_remote(ref, ref, bun_s.at[zz, h - 2], bun_r.at[zz, h - 2], to, head)

    def bundle_wait(zz, h):
        wait_recv(pairs.at[zz, h, pl.ds(0, 3)], bun_r.at[zz, h - 2], me, head)

    def column_own(h):
        start_remote(own.at[h, part_up], pairs.at[z, h, 0], up_s.at[z, h], col_r.at[z, h, 0], above, head)
        start_remote(own.at[h, part_dn], pairs.at[z, h, 1], dn_s.at[z, h], col_r.at[z, h, 1], below, head)

    def column_on(zz, h):
        start_remote(
            pairs.at[zz, h, 3 + part_up], pairs.at[zz, h, 0], up_s.at[zz, h], col_r.at[zz, h, 0], above, head
        )
        start_remote(
            pairs.at[zz, h, 3 + part_dn], pairs.at[zz, h, 1], dn_s.at[zz, h], col_r.at[zz, h, 1], below, head
        )

    def relay(zz, h):
        wait_recv(pairs.at[zz, h, 0], col_r.at[zz, h, 0], me, head)
        wait_recv(pairs.at[zz, h, 1], col_r.at[zz, h, 1], me, head)

        @pl.when(inner)
        def _():
            start_remote(
                pairs.at[zz, h, 0], pairs.at[zz, h, 2], rel_s.at[zz, h, 0], col_r.at[zz, h, 2], above, head
            )
            start_remote(
                pairs.at[zz, h, 1], pairs.at[zz, h, 2], rel_s.at[zz, h, 1], col_r.at[zz, h, 2], below, head
            )

    def opposite_wait(zz, h):
        wait_recv(pairs.at[zz, h, 2], col_r.at[zz, h, 2], me, head)

    ring_own(0, right)
    ring_own(1, left)
    column_own(2)
    column_own(3)
    ring_own(2, right)
    ring_own(3, left)
    column_own(0)
    column_own(1)
    relay(z, 2)
    relay(z, 3)
    opposite_wait(z, 2)
    bundle_on(z, 2, right)
    opposite_wait(z, 3)
    bundle_on(z, 3, left)

    def lap(s, last):
        zr, zl = lax.rem(z + nz - s, nz), lax.rem(z + s, nz)
        pr, pml = lax.rem(z + nz - s + 1, nz), lax.rem(z + s - 1, nz)
        for h, zz, to in ((0, zr, right), (1, zl, left)):
            ring_wait(zz, h)
            if not last:
                ring_on(zz, h, to)
            column_on(zz, h)
        for h, zz, to in ((2, zr, right), (3, zl, left)):
            ring_wait(zz, h)
            if not last:
                ring_on(zz, h, to)
        for h, zz in ((0, pr), (1, pml)):
            relay(zz, h)
        for h, zz, to in ((2, zr, right), (3, zl, left)):
            bundle_wait(zz, h)
            if not last:
                bundle_on(zz, h, to)

    lap(1, False)
    small_rows(nz, head, fin_own, fin, fsem)
    scan_rows(nz, head, state, fin, bufs, False)
    lap(2, False)
    small_finish(nz, head, fin_own, fin, fsem)
    scan_spread(nz, head, fin, state_in, bufs, False)

    @pl.loop(3, nz - 1)
    def _(s):
        lap(s, False)

    lap(nz - 1, True)
    for h, zz in ((0, lax.rem(z + 1, nz)), (1, lax.rem(z + nz - 1, nz))):
        relay(zz, h)
    scan_finish(nz, head, state_in, bufs)
    small_drain(nz, head, fin_own, fin, fsem)

    @pl.loop(0, nz)
    def _(zz):
        for h in range(2):
            opposite_wait(zz, h)
            wait_send(pairs.at[zz, h, 0], up_s.at[zz, h], me, head)
            wait_send(pairs.at[zz, h, 1], dn_s.at[zz, h], me, head)

            @pl.when(inner)
            def _():
                wait_send(pairs.at[zz, h, 0], rel_s.at[zz, h, 0], me, head)
                wait_send(pairs.at[zz, h, 1], rel_s.at[zz, h, 1], me, head)

    for h in range(2, HL):
        wait_send(pairs.at[z, h, 0], up_s.at[z, h], me, head)
        wait_send(pairs.at[z, h, 1], dn_s.at[z, h], me, head)

        @pl.when(inner)
        def _():
            wait_send(pairs.at[z, h, 0], rel_s.at[z, h, 0], me, head)
            wait_send(pairs.at[z, h, 1], rel_s.at[z, h, 1], me, head)

    @pl.loop(0, nz - 1)
    def _(s):
        for h in range(HL):
            zz = lax.rem(z + nz - s, nz) if h % 2 == 0 else lax.rem(z + s, nz)
            wait_send(pairs.at[zz, h, pl.ds(3, 2)], ring_s.at[zz, h], me, head)
            if h >= 2:
                wait_send(pairs.at[zz, h, pl.ds(0, 3)], bun_s.at[zz, h - 2], me, head)


def exchange(nz, own, state, fin):
    full = pl.BlockSpec(memory_space=pltpu.VMEM)
    hbm = pl.BlockSpec(memory_space=pl.ANY)
    sem = pltpu.SemaphoreType.DMA
    return pl.pallas_call(
        functools.partial(exchange_kernel, nz),
        out_shape=(
            jax.ShapeDtypeStruct((nz, HL, 5, 2, B, B), BF16),
            jax.ShapeDtypeStruct((HL * B, B), BF16),
            jax.ShapeDtypeStruct((NY, nz, 2 * HL, B), F32),
        ),
        in_specs=[hbm, full, full],
        out_specs=(hbm, full, full),
        scratch_shapes=[
            sem((nz, HL)),
            sem((nz, HL)),
            sem((nz, 2)),
            sem((nz, 2)),
            sem((nz, HL)),
            sem((nz, HL)),
            sem((nz, HL, 3)),
            sem((nz, HL, 2)),
            sem((5, max(nz, NY))),
        ]
        + scan_scratch(nz),
        compiler_params=pltpu.CompilerParams(collective_id=0, has_side_effects=True),
    )(own.reshape(HL, 2, 2, B, B), state, fin)


def query_kernel(
    nz, lists, count, own, pairs, lin, dec, state_in, dq_out, stats, lo_out, sq_out, sc, dpc, mx, ls, acc, tmp
):
    y, z = place(nz)
    n = count[0]
    causal = iota(0) >= iota(1)
    for h in range(HL):
        s = jnp.where(causal, mm_t(own[h, 1, 0], own[h, 0, 0]) * SCALE, NEG)
        sc[NSEL, h] = s
        mx[h] = s

    def where_is(e):
        j = lists[0, e]
        r, zz = j // nz, lax.rem(j, nz)
        return zz, jnp.where(r == y, 3, slot_of(r, y))

    def scores(e, _):
        zz, slot = where_is(e)
        for h in range(HL):
            s = mm_t(own[h, 1, 0], pairs[zz, h, slot, 0]) * SCALE
            sc[e, h] = s
            mx[h] = jnp.maximum(mx[h], s)
        return 0

    lax.fori_loop(0, n, scores, 0)
    for h in range(HL):
        m = jnp.broadcast_to(jnp.max(mx[h], axis=1, keepdims=True), (B, B))
        mx[h] = m
        p = jnp.exp(sc[NSEL, h] - m)
        sc[NSEL, h] = p
        ls[h] = p
        acc[h] = mm(p.astype(BF16), own[h, 0, 1])
        dpc[NSEL, h] = mm_t(own[h, 1, 1], own[h, 0, 1])

    def values(e, _):
        zz, slot = where_is(e)
        for h in range(HL):
            p = jnp.exp(sc[e, h] - mx[h])
            sc[e, h] = p
            ls[h] = ls[h] + p
            v = pairs[zz, h, slot, 1]
            acc[h] = acc[h] + mm(p.astype(BF16), v)
            dpc[e, h] = mm_t(own[h, 1, 1], v)
        return 0

    lax.fori_loop(0, n, values, 0)
    stats[...] = jnp.zeros_like(stats)
    lane = lax.broadcasted_iota(jnp.int32, (1, B), 1)

    def mark(e, row):
        return jnp.where(lane == lists[0, e], 1.0, row)

    stats[2 * HL : 2 * HL + 1, :] = lax.fori_loop(0, n, mark, jnp.zeros((1, B), F32))
    inv = []
    for h in range(HL):
        total = jnp.sum(ls[h], axis=1, keepdims=True)
        inv.append(1.0 / total)
        out = acc[h] * inv[h]
        delta = jnp.sum(own[h, 1, 1].astype(F32) * out, axis=1, keepdims=True)
        stats[h : h + 1, :] = row_of(mx[h][:, 0:1] + jnp.log(total))
        stats[HL + h : HL + h + 1, :] = row_of(delta)
        delta = jnp.broadcast_to(delta, (B, B))
        mx[h] = delta
        ds = (sc[NSEL, h] * (dpc[NSEL, h] - delta)).astype(BF16)
        acc[h] = mm(ds, own[h, 0, 0])

    def back(e, _):
        zz, slot = where_is(e)
        for h in range(HL):
            ds = (sc[e, h] * (dpc[e, h] - mx[h])).astype(BF16)
            acc[h] = acc[h] + mm(ds, pairs[zz, h, slot, 0])
        return 0

    lax.fori_loop(0, n, back, 0)
    for h in range(HL):
        tmp[pl.ds(h, B, stride=HL), :] = acc[h] * (inv[h] * SCALE)
    dq_out[...] = tmp[...].astype(BF16)

    run = running_of(dec[...])
    squares = jnp.zeros((B, 1), F32)
    for h in range(HL):
        row = run[h : h + 1]
        col = col_of(row)
        w = (mm_t(lin[h, 0], lin[h, 1]) * within_of(row, col)).astype(BF16)
        lo = mm(w, lin[h, 2]) + jnp.exp(col) * mm(lin[h, 0], state_in[pl.ds(h * B, B), :])
        lo_out[h] = lo
        squares = squares + jnp.sum(lo * lo, axis=1, keepdims=True)
    sq_out[...] = jnp.broadcast_to(row_of(squares), (8, B))


def queries(nz, lists, count, own, pairs, lin, dec, state_in):
    full = pl.BlockSpec(memory_space=pltpu.VMEM)
    smem = pl.BlockSpec(memory_space=pltpu.SMEM)
    return pl.pallas_call(
        functools.partial(query_kernel, nz),
        out_shape=(
            jax.ShapeDtypeStruct((HL * B, B), BF16),
            jax.ShapeDtypeStruct((16, B), F32),
            jax.ShapeDtypeStruct((HL, B, B), F32),
            jax.ShapeDtypeStruct((8, B), F32),
        ),
        in_specs=[smem, smem] + [full] * 5,
        out_specs=(full,) * 4,
        scratch_shapes=[
            pltpu.VMEM((NSEL + 1, HL, B, B), F32),
            pltpu.VMEM((NSEL + 1, HL, B, B), F32),
            pltpu.VMEM((HL, B, B), F32),
            pltpu.VMEM((HL, B, B), F32),
            pltpu.VMEM((HL, B, B), F32),
            pltpu.VMEM((HL * B, B), F32),
        ],
        compiler_params=pltpu.CompilerParams(vmem_limit_bytes=56 << 20),
    )(lists, count, own.reshape(HL, 2, 2, B, B), pairs, lin, dec, state_in)


def tail_kernel(
    nz,
    nh,
    own,
    pairs,
    lin,
    dec,
    fin,
    gain,
    stats_own,
    lo_in,
    sq_in,
    dk_out,
    dv_out,
    cot_out,
    rev_out,
    stats,
    dk,
    dv,
    cot,
    local,
    hbuf,
    isrc,
    hsem,
    ssem,
    *bufs,
):
    head = lax.axis_index("head")
    y, z = place(nz)
    me = y * nz + z
    greet(nz, head, nh)
    small_start(nz, head, stats_own, stats, ssem)

    def heads_start(k, src):
        for d in range(1, nh):
            hh = lax.rem(head + d, nh)
            start_remote(src, hbuf.at[k, head], hsem.at[2 * k, hh], hsem.at[2 * k + 1, head], me, hh)

    def heads_total(k, src):
        total = src[...]
        for d in range(1, nh):
            hh = lax.rem(head + d, nh)
            wait_recv(hbuf.at[k, hh], hsem.at[2 * k + 1, hh], me, head)
            total = total + hbuf[k, hh]
            wait_send(src, hsem.at[2 * k, hh], me, head)
        return total[0:1]

    heads_start(0, sq_in)
    for h in range(HL):
        keep = iota(0) <= iota(1)
        s = mm_t(own[h, 0, 0], own[h, 1, 0]) * SCALE
        p = jnp.where(keep, jnp.exp(jnp.where(keep, s - stats_own[h : h + 1, :], 0.0)), 0.0)
        dv[h] = mm(p.astype(BF16), own[h, 1, 1])
        dp = mm_t(own[h, 0, 1], own[h, 1, 1])
        ds = (p * (dp - stats_own[HL + h : HL + h + 1, :])).astype(BF16)
        dk[h] = mm(ds, own[h, 1, 0])

    lane = lax.broadcasted_iota(jnp.int32, (1, B), 1)

    def one(i, slot):
        r, zz = i // nz, lax.rem(i, nz)
        here = jnp.sum(jnp.where(lane == me, stats[r, zz, 2 * HL : 2 * HL + 1, :], 0.0), axis=1, keepdims=True)
        for h in range(HL):
            lse = jnp.where(here > 0.5, stats[r, zz, h : h + 1, :], BIG)
            q, g = pairs[zz, h, slot, 0], pairs[zz, h, slot, 1]
            s = mm_t(own[h, 0, 0], q) * SCALE
            p = jnp.exp(s - lse)
            dv[h] = dv[h] + mm(p.astype(BF16), g)
            dp = mm_t(own[h, 0, 1], g)
            ds = (p * (dp - stats[r, zz, HL + h : HL + h + 1, :])).astype(BF16)
            dk[h] = dk[h] + mm(ds, q)

    small_rows(nz, head, stats_own, stats, ssem)

    @pl.loop(me + 1, (y + 1) * nz)
    def _(i):
        one(i, 4)

    small_finish(nz, head, stats_own, stats, ssem)

    @pl.loop((y + 1) * nz, NY * nz)
    def _(i):
        one(i, slot_of(i // nz, y))

    partial = jnp.zeros((B, 1), F32)
    for h in range(HL):
        dk_out[h] = (dk[h] * SCALE).astype(BF16)
        dv_out[h] = dv[h].astype(BF16)
        c = (dv[h] + own[h, 1, 1].astype(F32)) * gain[h : h + 1, :]
        cot[h] = c
        partial = partial + jnp.sum(c * lo_in[h], axis=1, keepdims=True)
    isrc[...] = jnp.broadcast_to(row_of(partial), (8, B))
    heads_start(1, isrc)
    width = HL * nh * B
    root = jnp.sqrt(heads_total(0, sq_in) / width + EPS)
    inner = heads_total(1, isrc)
    factor = col_of(inner / (width * root * root * root))
    inv = col_of(1.0 / root)
    run = running_of(dec[...])
    leading = jnp.exp(run)
    for h in range(HL):
        lc = (cot[h] * inv - lo_in[h] * factor).astype(BF16)
        cot_out[h] = lc
        q = (lin[h, 0].astype(F32) * col_of(leading[h : h + 1])).astype(BF16)
        local[pl.ds(h * B, B), :] = t_mm(q, lc).astype(BF16)
    scan_start(nz, head, local, bufs)
    scan_rows(nz, head, local, fin, bufs, True)
    scan_spread(nz, head, fin, rev_out, bufs, True)
    scan_finish(nz, head, rev_out, bufs)
    small_drain(nz, head, stats_own, stats, ssem)


def tail(nz, nh, own, pairs, lin, dec, fin, gain, stats, lo, sq):
    full = pl.BlockSpec(memory_space=pltpu.VMEM)
    sem = pltpu.SemaphoreType.DMA
    return pl.pallas_call(
        functools.partial(tail_kernel, nz, nh),
        out_shape=(
            jax.ShapeDtypeStruct((HL, B, B), BF16),
            jax.ShapeDtypeStruct((HL, B, B), BF16),
            jax.ShapeDtypeStruct((HL, B, B), BF16),
            jax.ShapeDtypeStruct((HL * B, B), BF16),
        ),
        in_specs=[full] * 9,
        out_specs=(full,) * 4,
        scratch_shapes=[
            pltpu.VMEM((NY, nz, 16, B), F32),
            pltpu.VMEM((HL, B, B), F32),
            pltpu.VMEM((HL, B, B), F32),
            pltpu.VMEM((HL, B, B), F32),
            pltpu.VMEM((HL * B, B), BF16),
            pltpu.VMEM((2, nh, 8, B), F32),
            pltpu.VMEM((8, B), F32),
            sem((4, nh)),
            sem((5, max(nz, NY))),
        ]
        + scan_scratch(nz),
        compiler_params=pltpu.CompilerParams(
            collective_id=1, has_side_effects=True, vmem_limit_bytes=56 << 20
        ),
    )(own.reshape(HL, 2, 2, B, B), pairs, lin, dec, fin, gain, stats, lo, sq)


def last_kernel(lin, dec, state_in, cot, rev, dk_in, dv_in, dq_o, dk_o, dv_o, sk_o, sv_o, tmp):
    run = running_of(dec[...])
    trail = jnp.exp(run[:, B - 1 : B] - run)
    keep = iota(0) <= iota(1)

    def put(ref, value):
        for h in range(HL):
            tmp[pl.ds(h, B, stride=HL), :] = value(h)
        ref[...] = tmp[...].astype(BF16)

    def dq(h):
        row = run[h : h + 1]
        col = col_of(row)
        pair = (mm_t(cot[h], lin[h, 2]) * within_of(row, col)).astype(BF16)
        return mm(pair, lin[h, 1]) + jnp.exp(col) * mm_t(cot[h], state_in[pl.ds(h * B, B), :])

    def within_t(h):
        row = run[h : h + 1]
        return jnp.where(keep, jnp.exp(jnp.where(keep, row - col_of(row), 0.0)), 0.0)

    def dk(h):
        pair = (mm_t(lin[h, 2], cot[h]) * within_t(h)).astype(BF16)
        return mm(pair, lin[h, 0]) + col_of(trail[h : h + 1]) * mm_t(lin[h, 2], rev[pl.ds(h * B, B), :])

    def dv(h):
        pair = (mm_t(lin[h, 1], lin[h, 0]) * within_t(h)).astype(BF16)
        return mm(pair, cot[h]) + col_of(trail[h : h + 1]) * mm(lin[h, 1], rev[pl.ds(h * B, B), :])

    put(dq_o, dq)
    put(dk_o, dk)
    put(dv_o, dv)
    put(sk_o, lambda h: dk_in[h].astype(F32))
    put(sv_o, lambda h: dv_in[h].astype(F32))


def last(lin, dec, state_in, cot, rev, dk, dv):
    full = pl.BlockSpec(memory_space=pltpu.VMEM)
    return pl.pallas_call(
        last_kernel,
        out_shape=(jax.ShapeDtypeStruct((HL * B, B), BF16),) * 5,
        in_specs=[full] * 7,
        out_specs=(full,) * 5,
        scratch_shapes=[pltpu.VMEM((HL * B, B), F32)],
    )(lin, dec, state_in, cot, rev, dk, dv)


def local(nz, nh, lin_q, lin_k, lin_v, decay, gain, soft_q, soft_k, soft_v, out_grad, lists, counts):
    flat = [a.reshape(B * HL, B) for a in (lin_q, lin_k, lin_v, soft_q, soft_k, soft_v, out_grad)]
    own, lin, state, fin_own = prep(flat, decay)
    pairs, state_in, fin = exchange(nz, own, state, fin_own)
    dq, stats, lo, sq = queries(nz, lists, counts, own, pairs, lin, decay, state_in)
    dk, dv, cot, rev = tail(nz, nh, own, pairs, lin, decay, fin, gain, stats, lo, sq)
    lin_dq, lin_dk, lin_dv, soft_dk, soft_dv = last(lin, decay, state_in, cot, rev, dk, dv)
    return tuple(a.reshape(B, HL, B) for a in (lin_dq, lin_dk, lin_dv, dq, soft_dk, soft_dv))


def solution(mesh):
    nz = mesh.shape["ctx"] // NY
    tokens = P("ctx", "head", None)
    in_specs = (
        (tokens,) * 3 + (P("head", "ctx"), P("head", None)) + (tokens,) * 4 + (P("ctx", None), P("ctx"))
    )
    return jax.shard_map(
        functools.partial(local, nz, mesh.shape["head"]),
        mesh=mesh,
        in_specs=in_specs,
        out_specs=(tokens,) * 6,
        check_vma=False,
    )
```

time: 773 us -> 197 us (0.25)
  waiting for transfers between devices: 256 us -> 0 us
  blocking collectives: 239 us -> 0 us
  Pallas kernels: 0 us -> 192 us
  local copies, waits for them, and re-layouts: 114 us -> 0 us
  other arithmetic: 53.3 us -> 0 us
  matrix products: 47 us -> 0 us
  starting transfers between devices: 45.2 us -> 0 us
  between operations: 15.6 us -> 1.3 us
    pallas_call x0 -> x5, Pallas kernels: none -> 192 us  [the longest x1 95 us: exchange(): pl.pallas_call(functools.partial(exchange_kernel, nz), out_shape=(jax.Sha...]
    unnamed x2 -> x0, blocking collectives: 188 us -> none
    all_to_all x2 -> x0, waiting for transfers between devices: 128 us -> none  [the longest x1 128 us: local(): lax.all_to_all(part_key, 'ctx', split_axis=0, concat_axis=0, tiled=True)]
    all_gather x4 -> x0, waiting for transfers between devices: 127 us -> none  [the longest x1 76.2 us: local(): lax.all_gather(soft_v, 'ctx', axis=0, tiled=True)]
    gather x4 -> x0, local copies, waits for them, and re-layouts: 68.5 us -> none  [the longest x1 30.5 us: local(): new_keys = jnp.where(usable, shard_piece[0][safe_index], empty_slot)]
    all_to_all x2 -> x0, starting transfers between devices: 45.1 us -> none  [the longest x1 38.5 us: local(): lax.all_to_all(part_key, 'ctx', split_axis=0, concat_axis=0, tiled=True)]
    dot_general x21 -> x0, matrix products: 43.1 us -> none  [the longest x1 7.43 us: local(): jnp.einsum('oe,exhd->oxhd', routing, remote_value, precision=exact_precis...]
    all_gather x1 -> x0, blocking collectives: 37.6 us -> none  [local(): lax.all_gather(block_lists, 'ctx', axis=0, tiled=True)]
  transfers between devices with their start and end apart: 6 -> 0, of which waited for: 3 -> 0; matrix products, arithmetic and copies ran while one was open for 19% -> 0% of each run, Pallas kernels for 0% -> 0%
where the time goes in v1:
time: 197 us; the launch traced here: 194 us
  Pallas kernels  192 us (97%)
    pallas_call x1, Pallas kernels, exchange(): pl.pallas_call(functools.partial(exchange_kernel, nz), out_shape=(jax.Sha...  95 us
    pallas_call x1, Pallas kernels, tail(): pl.pallas_call(functools.partial(tail_kernel, nz, nh), out_shape=(jax.Sha...  83.6 us
    pallas_call x1, Pallas kernels, queries(): pl.pallas_call(functools.partial(query_kernel, nz), out_shape=(jax.ShapeD...  7.49 us

profile of v1, /device:TPU:32, one launch (start us, length us, event | category | flops | bytes accessed | tf_op | source)
XLA Modules:
  0.0 193.5 jit_solution(8266696697035464403)
XLA Ops:
  1.3 2.8 %shard_map.154 = (bf16[4,4,128,128]{3,2,1,0:T(8,128)(2,1)}, bf16[4,3,128,128]{3,2,1,0:T(8,128)(2,1)}, bf16[512,128]{1,0:T(8,128)(2,1)}, f32[8,128]{1,0:T(8,128)}) custom-call(bf16[512,128]{1,0:T(8,128)(2,1)} %bitcast.17, bf16[512,128]{1,0:T(8,128)(2,1)} %bitcast.18, bf16[512,128]{1,0:T(8,128)(2,1)} %bitcast.19, bf16[512,128]{1,0:T(8,128)(2,1)} %bitcast.20, ...), custom_call_target="tpu_custom_call" | custom-call | tf_op jit(solution)/shard_map/pallas_call | solution.py:117
  4.1 95.0 %shard_map.155 = (bf16[8,4,5,2,128,128]{5,4,3,2,1,0:T(8,128)(2,1)}, bf16[512,128]{1,0:T(8,128)(2,1)}, f32[4,8,8,128]{3,2,1,0:T(8,128)}) custom-call(bf16[4,2,2,128,128]{4,3,2,1,0:T(8,128)(2,1)} %bitcast.14, bf16[512,128]{1,0:T(8,128)(2,1)} %get-tuple-element.28.state, f32[8,128]{1,0:T(8,128)} %get-tuple-element.29.fin_own), custom_call_target="tpu_custom_call" | custom-call | tf_op jit(solution)/shard_map/pallas_call | solution.py:425
  99.1 7.5 %shard_map.156 = (bf16[512,128]{1,0:T(8,128)(2,1)}, f32[16,128]{1,0:T(8,128)}, f32[4,128,128]{2,1,0:T(8,128)}, f32[8,128]{1,0:T(8,128)}) custom-call(s32[1,16]{1,0:T(1,128)} %lists.1, s32[1]{0:T(128)S(6)} %copy.17.count, bf16[4,2,2,128,128]{4,3,2,1,0:T(8,128)(2,1)} %bitcast.15, bf16[8,4,5,2,128,128]{5,4,3,2,1,0:T(8,128)(2,1)} %get-tuple-element.31.pairs, ...), custom_call_target="tpu_custom_call" | custom-call | tf_op jit(solution)/shard_map/pallas_call | solution.py:543
  106.5 83.6 %shard_map.157 = (bf16[4,128,128]{2,1,0:T(8,128)(2,1)}, bf16[4,128,128]{2,1,0:T(8,128)(2,1)}, bf16[4,128,128]{2,1,0:T(8,128)(2,1)}, bf16[512,128]{1,0:T(8,128)(2,1)}) custom-call(bf16[4,2,2,128,128]{4,3,2,1,0:T(8,128)(2,1)} %bitcast.16, bf16[8,4,5,2,128,128]{5,4,3,2,1,0:T(8,128)(2,1)} %get-tuple-element.31.pairs, ...), custom_call_target="tpu_custom_call" | custom-call | tf_op jit(solution)/shard_map/pallas_call | solution.py:680
  190.1 3.4 %shard_map.158 = (bf16[512,128]{1,0:T(8,128)(2,1)}, bf16[512,128]{1,0:T(8,128)(2,1)}, bf16[512,128]{1,0:T(8,128)(2,1)}, bf16[512,128]{1,0:T(8,128)(2,1)}, bf16[512,128]{1,0:T(8,128)(2,1)}) custom-call(bf16[4,3,128,128]{3,2,1,0:T(8,128)(2,1)} %get-tuple-element.26.lin, f32[4,128]{1,0:T(4,128)} %dec.7, bf16[512,128]{1,0:T(8,128)(2,1)} %get-tuple-element.30.state_in, ...), custom_call_target="tpu_custom_call" | custom-call | tf_op jit(solution)/shard_map/pallas_call | solution.py:745

commit v2 on v1

v2 whole, which is shorter than its diff:
```python
import functools

import jax
import jax.numpy as jnp
from jax import lax
from jax.experimental import pallas as pl
from jax.experimental.pallas import tpu as pltpu
from jax.sharding import PartitionSpec as P

NY = 4
HL = 4
B = 128
NSEL = 16
EPS = 1e-05
SCALE = 128 ** (-0.5)
NEG = -1e30
BIG = 1e30
F32 = jnp.float32
BF16 = jnp.bfloat16
MESH = pl.DeviceIdType.MESH
HIGH = lax.Precision.HIGHEST


def mm(a, b):
    return lax.dot_general(a, b, (((1,), (0,)), ((), ())), preferred_element_type=F32)


def mm_t(a, b):
    return lax.dot_general(a, b, (((1,), (1,)), ((), ())), preferred_element_type=F32)


def t_mm(a, b):
    return lax.dot_general(a, b, (((0,), (0,)), ((), ())), preferred_element_type=F32)


def iota(dim):
    return lax.broadcasted_iota(jnp.int32, (B, B), dim)


def col_of(row):
    return jnp.transpose(jnp.broadcast_to(row, (B, B)))


def row_of(col):
    return jnp.transpose(jnp.broadcast_to(col, (B, B)))[0:1]


def running_of(decay):
    upper = (iota(0) <= iota(1)).astype(F32)
    return lax.dot_general(
        decay, upper, (((1,), (0,)), ((), ())), precision=HIGH, preferred_element_type=F32
    )


def within_of(row, col):
    keep = iota(0) >= iota(1)
    return jnp.where(keep, jnp.exp(jnp.where(keep, col - row, 0.0)), 0.0)


def slot_of(r, y):
    return jnp.where(lax.rem(y + 3, NY) == r, 0, jnp.where(lax.rem(y + 1, NY) == r, 1, 2))


def place(nz):
    own = lax.axis_index("ctx")
    return own // nz, lax.rem(own, nz)


def start_remote(src, dst, send, recv, ctx, head):
    pltpu.make_async_remote_copy(
        src_ref=src, dst_ref=dst, send_sem=send, recv_sem=recv, device_id=(ctx, head), device_id_type=MESH
    ).start()


def wait_recv(ref, recv, ctx, head):
    pltpu.make_async_remote_copy(
        src_ref=ref, dst_ref=ref, send_sem=recv, recv_sem=recv, device_id=(ctx, head), device_id_type=MESH
    ).wait_recv()


def wait_send(ref, send, ctx, head):
    pltpu.make_async_remote_copy(
        src_ref=ref, dst_ref=ref, send_sem=send, recv_sem=send, device_id=(ctx, head), device_id_type=MESH
    ).wait_send()


def prep_kernel(nz, lists, count, lq, lk, lv, sq, sk, sv, og, dec, own, lin, state, fin, bias, mask, tmp):
    def heads(ref, store):
        tmp[...] = ref[...].astype(F32)
        for h in range(HL):
            store(h, tmp[pl.ds(h, B, stride=HL), :].astype(BF16))

    def into(dst, a):
        def store(h, value):
            dst[h, a] = value

        return store

    y, _ = place(nz)
    bias[...] = jnp.full_like(bias, NEG)
    lane = lax.broadcasted_iota(jnp.int32, (8, B), 1)

    def mark(e, row):
        j = lists[0, e]
        r = j // nz
        k = jnp.where(r == y, 3, slot_of(r, y))
        bias[k, pl.ds(lax.rem(j, nz), 1), :] = jnp.zeros((1, B), F32)
        return jnp.where(lane == j, 1.0, row)

    mask[...] = lax.fori_loop(0, count[0], mark, jnp.zeros((8, B), F32))
    heads(sk, into(own, 0))
    heads(sv, into(own, 1))
    heads(sq, into(own, 2))
    heads(og, into(own, 3))
    heads(lq, into(lin, 0))
    heads(lk, into(lin, 1))
    heads(lv, into(lin, 2))
    run = running_of(dec[...])
    finish = run[:, B - 1 : B]
    fin[...] = jnp.concatenate([jnp.broadcast_to(finish, (HL, B))] * 2, axis=0)
    trailing = jnp.exp(finish - run)
    for h in range(HL):
        k = lin[h, 1].astype(F32) * col_of(trailing[h : h + 1])
        state[pl.ds(h * B, B), :] = t_mm(k.astype(BF16), lin[h, 2]).astype(BF16)


def prep(nz, lists, counts, arrays, decay):
    full = pl.BlockSpec(memory_space=pltpu.VMEM)
    smem = pl.BlockSpec(memory_space=pltpu.SMEM)
    return pl.pallas_call(
        functools.partial(prep_kernel, nz),
        out_shape=(
            jax.ShapeDtypeStruct((HL, 4, B, B), BF16),
            jax.ShapeDtypeStruct((HL, 3, B, B), BF16),
            jax.ShapeDtypeStruct((HL * B, B), BF16),
            jax.ShapeDtypeStruct((2 * HL, B), F32),
            jax.ShapeDtypeStruct((4, nz, B), F32),
            jax.ShapeDtypeStruct((8, B), F32),
        ),
        in_specs=[smem, smem] + [full] * 8,
        out_specs=(full,) * 6,
        scratch_shapes=[pltpu.VMEM((HL * B, B), F32)],
    )(lists, counts, *arrays, decay)


def scan_scratch(nz):
    rs = HL * B // nz
    return [
        pltpu.VMEM((nz, rs, B), BF16),
        pltpu.VMEM((nz, rs, B), F32),
        pltpu.VMEM((NY, rs, B), F32),
        pltpu.VMEM((rs, B), F32),
        pltpu.VMEM((nz, rs, B), BF16),
        pltpu.SemaphoreType.DMA((6, nz)),
        pltpu.SemaphoreType.DMA((2,)),
    ]


def scan_start(nz, head, local, bufs):
    zbuf, sems, lsem = bufs[0], bufs[5], bufs[6]
    rs = HL * B // nz
    y, z = place(nz)
    for d in range(1, nz):
        zz = lax.rem(z + d, nz)
        start_remote(
            local.at[pl.ds(zz * rs, rs)], zbuf.at[z], sems.at[0, zz], sems.at[1, z], y * nz + zz, head
        )
    pltpu.make_async_copy(local.at[pl.ds(z * rs, rs)], zbuf.at[z], lsem.at[0]).start()


def scan_rows(nz, head, local, fin, bufs, reverse):
    zbuf, ebuf, tbuf, tsrc, _, sems, lsem = bufs
    rs = HL * B // nz
    y, z = place(nz)
    own = y * nz + z
    hz = z * rs // B
    pltpu.make_async_copy(local.at[pl.ds(z * rs, rs)], zbuf.at[z], lsem.at[0]).wait()
    for d in range(1, nz):
        zz = lax.rem(z + d, nz)
        wait_recv(zbuf.at[zz], sems.at[1, zz], own, head)

    total = jnp.zeros((rs, B), F32)
    for lap in range(nz):
        m = nz - 1 - lap if reverse else lap
        ebuf[m] = total
        total = total * jnp.exp(fin[y, m, pl.ds(hz, 1), :]) + zbuf[m].astype(F32)
    tsrc[...] = total
    for d in range(1, NY):
        yy = lax.rem(y + d, NY)
        start_remote(tsrc, tbuf.at[y], sems.at[2, yy], sems.at[3, y], yy * nz + z, head)
    for d in range(1, nz):
        zz = lax.rem(z + d, nz)
        wait_send(zbuf.at[0], sems.at[0, zz], own, head)


def scan_spread(nz, head, fin, out, bufs, reverse):
    _, ebuf, tbuf, tsrc, sbuf, sems, lsem = bufs
    rs = HL * B // nz
    y, z = place(nz)
    own = y * nz + z
    hz = z * rs // B
    for d in range(1, NY):
        yy = lax.rem(y + d, NY)
        wait_recv(tbuf.at[yy], sems.at[3, yy], own, head)
        wait_send(tsrc, sems.at[2, yy], own, head)
    carry = jnp.zeros((rs, B), F32)
    for lap in range(NY):
        r = NY - 1 - lap if reverse else lap
        use = (r > y) if reverse else (r < y)
        span = jnp.zeros((1, B), F32)
        for m in range(nz):
            span = span + fin[r, m, pl.ds(hz, 1), :]
        carry = jnp.where(use, carry * jnp.exp(span) + tbuf[r], carry)
    for lap in range(nz):
        m = nz - 1 - lap if reverse else lap
        sbuf[m] = (ebuf[m] + carry).astype(BF16)
        carry = carry * jnp.exp(fin[y, m, pl.ds(hz, 1), :])
    for d in range(1, nz):
        zz = lax.rem(z + d, nz)
        start_remote(
            sbuf.at[zz], out.at[pl.ds(z * rs, rs)], sems.at[4, zz], sems.at[5, z], y * nz + zz, head
        )
    pltpu.make_async_copy(sbuf.at[z], out.at[pl.ds(z * rs, rs)], lsem.at[1]).start()


def scan_finish(nz, head, out, bufs):
    sbuf, sems, lsem = bufs[4], bufs[5], bufs[6]
    rs = HL * B // nz
    y, z = place(nz)
    own = y * nz + z
    for d in range(1, nz):
        zz = lax.rem(z + d, nz)
        wait_recv(out.at[pl.ds(zz * rs, rs)], sems.at[5, zz], own, head)
        wait_send(sbuf.at[zz], sems.at[4, zz], own, head)
    pltpu.make_async_copy(sbuf.at[z], out.at[pl.ds(z * rs, rs)], lsem.at[1]).wait()


def small_start(nz, head, src, dst, sems):
    y, z = place(nz)
    for d in range(1, nz):
        zz = lax.rem(z + d, nz)
        start_remote(src, dst.at[y, z], sems.at[0, zz], sems.at[1, z], y * nz + zz, head)
    pltpu.make_async_copy(src, dst.at[y, z], sems.at[2, 0]).start()


def small_rows(nz, head, src, dst, sems):
    y, z = place(nz)
    own = y * nz + z
    for d in range(1, nz):
        zz = lax.rem(z + d, nz)
        wait_recv(dst.at[y, zz], sems.at[1, zz], own, head)
    pltpu.make_async_copy(src, dst.at[y, z], sems.at[2, 0]).wait()
    for d in range(1, NY):
        yy = lax.rem(y + d, NY)
        start_remote(dst.at[y], dst.at[y], sems.at[3, yy], sems.at[4, y], yy * nz + z, head)


def small_finish(nz, head, src, dst, sems):
    y, z = place(nz)
    own = y * nz + z
    for d in range(1, NY):
        yy = lax.rem(y + d, NY)
        wait_recv(dst.at[yy], sems.at[4, yy], own, head)


def small_drain(nz, head, src, dst, sems):
    y, z = place(nz)
    own = y * nz + z
    for d in range(1, nz):
        zz = lax.rem(z + d, nz)
        wait_send(src, sems.at[0, zz], own, head)
    for d in range(1, NY):
        yy = lax.rem(y + d, NY)
        wait_send(dst.at[y], sems.at[3, yy], own, head)


def greet(nz, head, nh):
    y, z = place(nz)
    barrier = pltpu.get_barrier_semaphore()
    for d in range(1, nz):
        pl.semaphore_signal(
            barrier, inc=1, device_id=(y * nz + lax.rem(z + d, nz), head), device_id_type=MESH
        )
    for d in range(1, NY):
        pl.semaphore_signal(
            barrier, inc=1, device_id=(lax.rem(y + d, NY) * nz + z, head), device_id_type=MESH
        )
    for d in range(1, nh):
        pl.semaphore_signal(
            barrier, inc=1, device_id=(y * nz + z, lax.rem(head + d, nh)), device_id_type=MESH
        )
    pl.semaphore_wait(barrier, nz - 1 + NY - 1 + nh - 1)


def fused_kernel(
    nz,
    nh,
    own,
    lin,
    dec,
    gain,
    state,
    fin_own,
    bias,
    mask,
    dq_out,
    dk_out,
    dv_out,
    cot_out,
    rev_out,
    state_in,
    pairs,
    a1,
    a2,
    mx,
    ls,
    acc,
    dv,
    dkq,
    lcol,
    dcol,
    lo,
    cot,
    rev_local,
    fin,
    stats_own,
    stats,
    hbuf,
    hsrc,
    ring_s,
    ring_r,
    bun_s,
    bun_r,
    up_s,
    dn_s,
    col_r,
    rel_s,
    fsem,
    ssem,
    hsem,
    *scans,
):
    fwd, bwd = scans[: len(scans) // 2], scans[len(scans) // 2 :]
    head = lax.axis_index("head")
    y, z = place(nz)
    me = y * nz + z
    right, left = y * nz + lax.rem(z + 1, nz), y * nz + lax.rem(z + nz - 1, nz)
    above, below = lax.rem(y + 1, NY) * nz + z, lax.rem(y + NY - 1, NY) * nz + z
    part_up = jnp.where(y < NY - 1, 0, 1)
    part_dn = jnp.where(y > 0, 1, 0)
    inner_row = (y == 1) | (y == 2)
    greet(nz, head, nh)
    small_start(nz, head, fin_own, fin, fsem)
    scan_start(nz, head, state, fwd)

    def ring_own(h, to):
        start_remote(own.at[h], pairs.at[z, h, pl.ds(3, 2)], ring_s.at[z, h], ring_r.at[z, h], to, head)

    def ring_on(zz, h, to):
        ref = pairs.at[zz, h, pl.ds(3, 2)]
        start_remote(ref, ref, ring_s.at[zz, h], ring_r.at[zz, h], to, head)

    def ring_wait(zz, h):
        wait_recv(pairs.at[zz, h, pl.ds(3, 2)], ring_r.at[zz, h], me, head)

    def bundle_on(zz, h, to):
        ref = pairs.at[zz, h, pl.ds(0, 3)]
        start_remote(ref, ref, bun_s.at[zz, h - 2], bun_r.at[zz, h - 2], to, head)

    def bundle_wait(zz, h):
        wait_recv(pairs.at[zz, h, pl.ds(0, 3)], bun_r.at[zz, h - 2], me, head)

    def column_own(h):
        start_remote(own.at[h, part_up], pairs.at[z, h, 0], up_s.at[z, h], col_r.at[z, h, 0], above, head)
        start_remote(own.at[h, part_dn], pairs.at[z, h, 1], dn_s.at[z, h], col_r.at[z, h, 1], below, head)

    def column_on(zz, h):
        start_remote(
            pairs.at[zz, h, 3 + part_up], pairs.at[zz, h, 0], up_s.at[zz, h], col_r.at[zz, h, 0], above, head
        )
        start_remote(
            pairs.at[zz, h, 3 + part_dn], pairs.at[zz, h, 1], dn_s.at[zz, h], col_r.at[zz, h, 1], below, head
        )

    def relay(zz, h):
        wait_recv(pairs.at[zz, h, 0], col_r.at[zz, h, 0], me, head)
        wait_recv(pairs.at[zz, h, 1], col_r.at[zz, h, 1], me, head)

        @pl.when(inner_row)
        def _():
            start_remote(
                pairs.at[zz, h, 0], pairs.at[zz, h, 2], rel_s.at[zz, h, 0], col_r.at[zz, h, 2], above, head
            )
            start_remote(
                pairs.at[zz, h, 1], pairs.at[zz, h, 2], rel_s.at[zz, h, 1], col_r.at[zz, h, 2], below, head
            )

    def opposite_wait(zz, h):
        wait_recv(pairs.at[zz, h, 2], col_r.at[zz, h, 2], me, head)

    def diagonal(h):
        s = jnp.where(iota(0) >= iota(1), mm_t(own[h, 1, 0], own[h, 0, 0]) * SCALE, NEG)
        m = jnp.broadcast_to(jnp.max(s, axis=1, keepdims=True), (B, B))
        p = jnp.exp(s - m)
        mx[h] = m
        ls[h] = p
        acc[h] = mm(p.astype(BF16), own[h, 0, 1])

    def block(zz, h, with_row):
        scores, values = [], []
        for k, off in ((0, NY - 1), (1, 1), (2, 2)):
            t = jnp.where(lax.rem(y + off, NY) < y, 1, 0)
            v = pairs[zz, h, k, 1]
            s = mm_t(own[h, t, 0], pairs[zz, h, k, 0]) * SCALE
            a1[zz, h, k] = s
            a2[zz, h, k] = mm_t(own[h, t, 1], v)
            scores.append(s + bias[k, pl.ds(zz, 1), :])
            values.append(v)
        if with_row:
            t = jnp.where(zz < z, 1, 0)
            v = pairs[zz, h, 4 - t, 1]
            s = mm_t(own[h, t, 0], pairs[zz, h, 4 - t, 0]) * SCALE
            a1[zz, h, 3] = s
            a2[zz, h, 3] = mm_t(own[h, t, 1], v)
            scores.append(s + bias[3, pl.ds(zz, 1), :])
            values.append(v)
        top = functools.reduce(jnp.maximum, scores)
        m = jnp.maximum(mx[h], jnp.broadcast_to(jnp.max(top, axis=1, keepdims=True), (B, B)))
        scale = jnp.exp(mx[h] - m)
        probs = [jnp.exp(s - m) for s in scores]
        mx[h] = m
        ls[h] = ls[h] * scale + functools.reduce(jnp.add, probs)
        low = jnp.concatenate([p.astype(BF16) for p in probs], axis=1)
        acc[h] = acc[h] * scale + mm(low, jnp.concatenate(values, axis=0))

    ring_own(0, right)
    ring_own(1, left)
    column_own(2)
    column_own(3)
    ring_own(2, right)
    ring_own(3, left)
    column_own(0)
    column_own(1)
    for h in range(HL):
        diagonal(h)

    def at(s, h):
        return lax.rem(z + nz - s, nz) if h % 2 == 0 else lax.rem(z + s, nz)

    def to_next(h):
        return right if h % 2 == 0 else left

    def lap(s, first=False, second=False, last=False):
        for h in range(HL):
            ring_wait(at(s, h), h)
            if not last:
                ring_on(at(s, h), h, to_next(h))
            if h < 2:
                column_on(at(s, h), h)
        if first:
            relay(z, 2)
            relay(z, 3)
            for h in (2, 3):
                opposite_wait(z, h)
                bundle_on(z, h, to_next(h))
        for h in (0, 1):
            relay(at(s - 1, h), h)
        if first:
            for h in (2, 3):
                block(z, h, False)
        for h in (2, 3):
            bundle_wait(at(s, h), h)
            if not last:
                bundle_on(at(s, h), h, to_next(h))
        for h in (2, 3):
            block(at(s, h), h, True)
        if not first:
            for h in (0, 1):
                opposite_wait(at(s - 2, h), h)
            for h in (0, 1):
                block(at(s - 2, h), h, not second)

    lap(1, first=True)
    small_rows(nz, head, fin_own, fin, fsem)
    scan_rows(nz, head, state, fin, fwd, False)
    lap(2, second=True)
    small_finish(nz, head, fin_own, fin, fsem)
    scan_spread(nz, head, fin, state_in, fwd, False)

    @pl.loop(3, nz - 1)
    def _(s):
        lap(s)

    lap(nz - 1, last=True)
    for h in (0, 1):
        relay(at(nz - 1, h), h)
    for s in (nz - 2, nz - 1):
        for h in (0, 1):
            opposite_wait(at(s, h), h)
            block(at(s, h), h, True)

    stats_own[...] = jnp.zeros_like(stats_own)
    stats_own[2 * HL : 2 * HL + 1, :] = mask[0:1, :]
    for h in range(HL):
        total = jnp.sum(ls[h], axis=1, keepdims=True)
        lse = mx[h] + jnp.log(total)
        delta = jnp.sum(own[h, 1, 1].astype(F32) * acc[h], axis=1, keepdims=True) / total
        delta = jnp.broadcast_to(delta, (B, B))
        lcol[h] = lse
        dcol[h] = delta
        stats_own[h : h + 1, :] = jnp.transpose(lse)[0:1]
        stats_own[HL + h : HL + h + 1, :] = jnp.transpose(delta)[0:1]
    small_start(nz, head, stats_own, stats, ssem)

    def heads_start(k):
        for d in range(1, nh):
            hh = lax.rem(head + d, nh)
            start_remote(hsrc.at[k], hbuf.at[k, head], hsem.at[2 * k, hh], hsem.at[2 * k + 1, head], me, hh)

    def heads_total(k):
        total = hsrc[k]
        for d in range(1, nh):
            hh = lax.rem(head + d, nh)
            wait_recv(hbuf.at[k, hh], hsem.at[2 * k + 1, hh], me, head)
            total = total + hbuf[k, hh]
            wait_send(hsrc.at[k], hsem.at[2 * k, hh], me, head)
        return total[0:1]

    scan_finish(nz, head, state_in, fwd)
    run = running_of(dec[...])
    squares = jnp.zeros((B, 1), F32)
    for h in range(HL):
        row = run[h : h + 1]
        col = col_of(row)
        w = (mm_t(lin[h, 0], lin[h, 1]) * within_of(row, col)).astype(BF16)
        o = mm(w, lin[h, 2]) + jnp.exp(col) * mm(lin[h, 0], state_in[pl.ds(h * B, B), :])
        lo[h] = o
        squares = squares + jnp.sum(o * o, axis=1, keepdims=True)
    hsrc[0] = jnp.broadcast_to(row_of(squares), (8, B))
    heads_start(0)
    for h in range(HL):
        keep = iota(0) <= iota(1)
        s = mm_t(own[h, 0, 0], own[h, 1, 0]) * SCALE
        p = jnp.where(keep, jnp.exp(jnp.where(keep, s - stats_own[h : h + 1, :], 0.0)), 0.0)
        dv[h] = mm(p.astype(BF16), own[h, 1, 1])
        dp = mm_t(own[h, 0, 1], own[h, 1, 1])
        ds = (p * (dp - stats_own[HL + h : HL + h + 1, :])).astype(BF16)
        dkq[0, h] = mm(ds, own[h, 1, 0])

    lane = lax.broadcasted_iota(jnp.int32, (1, B), 1)

    def value_block(i, k, slot):
        r, zz = i // nz, lax.rem(i, nz)
        here = jnp.sum(jnp.where(lane == me, stats[r, zz, 2 * HL : 2 * HL + 1, :], 0.0), axis=1, keepdims=True)
        for h in range(HL):
            lse = jnp.where(here > 0.5, stats[r, zz, h : h + 1, :], BIG)
            p = jnp.exp(a1[zz, h, k] - lse)
            a1[zz, h, k] = p
            dv[h] = dv[h] + mm(p.astype(BF16), pairs[zz, h, slot, 1])

    small_rows(nz, head, stats_own, stats, ssem)

    @pl.loop(me + 1, (y + 1) * nz)
    def _(i):
        value_block(i, 3, 4)

    small_finish(nz, head, stats_own, stats, ssem)

    @pl.loop((y + 1) * nz, NY * nz)
    def _(i):
        k = slot_of(i // nz, y)
        value_block(i, k, k)

    partial = jnp.zeros((B, 1), F32)
    for h in range(HL):
        dv_out[h] = dv[h].astype(BF16)
        c = (dv[h] + own[h, 1, 1].astype(F32)) * gain[h : h + 1, :]
        cot[h] = c
        partial = partial + jnp.sum(c * lo[h], axis=1, keepdims=True)
    hsrc[1] = jnp.broadcast_to(row_of(partial), (8, B))
    heads_start(1)
    width = HL * nh * B
    root = jnp.sqrt(heads_total(0) / width + EPS)

    for h in range(HL):
        s = jnp.where(iota(0) >= iota(1), mm_t(own[h, 1, 0], own[h, 0, 0]) * SCALE, NEG)
        p = jnp.exp(s - lcol[h])
        ds = (p * (mm_t(own[h, 1, 1], own[h, 0, 1]) - dcol[h])).astype(BF16)
        dkq[1, h] = mm(ds, own[h, 0, 0])

    def grads(lo_i, hi_i):
        @pl.loop(lo_i, jnp.minimum(hi_i, me))
        def _(i):
            r, zz = i // nz, lax.rem(i, nz)
            k = jnp.where(r == y, 3, slot_of(r, y))
            for h in range(HL):
                p = jnp.exp(a1[zz, h, k] + bias[k, pl.ds(zz, 1), :] - lcol[h])
                ds = (p * (a2[zz, h, k] - dcol[h])).astype(BF16)
                dkq[1, h] = dkq[1, h] + mm(ds, pairs[zz, h, k, 0])

        @pl.loop(jnp.maximum(lo_i, me + 1), hi_i)
        def _(i):
            r, zz = i // nz, lax.rem(i, nz)
            k = jnp.where(r == y, 3, slot_of(r, y))
            slot = jnp.where(r == y, 4, k)
            for h in range(HL):
                ds = (a1[zz, h, k] * (a2[zz, h, k] - stats[r, zz, HL + h : HL + h + 1, :])).astype(BF16)
                dkq[0, h] = dkq[0, h] + mm(ds, pairs[zz, h, slot, 0])

    inner = heads_total(1)
    factor = col_of(inner / (width * root * root * root))
    inv = col_of(1.0 / root)
    leading = jnp.exp(run)
    for h in range(HL):
        lc = (cot[h] * inv - lo[h] * factor).astype(BF16)
        cot_out[h] = lc
        q = (lin[h, 0].astype(F32) * col_of(leading[h : h + 1])).astype(BF16)
        rev_local[pl.ds(h * B, B), :] = t_mm(q, lc).astype(BF16)
    scan_start(nz, head, rev_local, bwd)
    n = NY * nz
    grads(0, n * 3 // 8)
    scan_rows(nz, head, rev_local, fin, bwd, True)
    grads(n * 3 // 8, n * 5 // 8)
    scan_spread(nz, head, fin, rev_out, bwd, True)
    grads(n * 5 // 8, n)
    for h in range(HL):
        dk_out[h] = (dkq[0, h] * SCALE).astype(BF16)
        dq_out[h] = (dkq[1, h] * SCALE).astype(BF16)
    scan_finish(nz, head, rev_out, bwd)

    small_drain(nz, head, fin_own, fin, fsem)
    small_drain(nz, head, stats_own, stats, ssem)

    @pl.loop(0, nz)
    def _(zz):
        for h in range(2):
            wait_send(pairs.at[zz, h, 0], up_s.at[zz, h], me, head)
            wait_send(pairs.at[zz, h, 1], dn_s.at[zz, h], me, head)

            @pl.when(inner_row)
            def _():
                wait_send(pairs.at[zz, h, 0], rel_s.at[zz, h, 0], me, head)
                wait_send(pairs.at[zz, h, 1], rel_s.at[zz, h, 1], me, head)

    for h in range(2, HL):
        wait_send(pairs.at[z, h, 0], up_s.at[z, h], me, head)
        wait_send(pairs.at[z, h, 1], dn_s.at[z, h], me, head)

        @pl.when(inner_row)
        def _():
            wait_send(pairs.at[z, h, 0], rel_s.at[z, h, 0], me, head)
            wait_send(pairs.at[z, h, 1], rel_s.at[z, h, 1], me, head)

    @pl.loop(0, nz - 1)
    def _(s):
        for h in range(HL):
            zz = at(s, h)
            wait_send(pairs.at[zz, h, pl.ds(3, 2)], ring_s.at[zz, h], me, head)
            if h >= 2:
                wait_send(pairs.at[zz, h, pl.ds(0, 3)], bun_s.at[zz, h - 2], me, head)


def fused(nz, nh, own, lin, decay, gain, state, fin, bias, mask):
    full = pl.BlockSpec(memory_space=pltpu.VMEM)
    sem = pltpu.SemaphoreType.DMA
    per_head = pltpu.VMEM((HL, B, B), F32)
    return pl.pallas_call(
        functools.partial(fused_kernel, nz, nh),
        out_shape=(jax.ShapeDtypeStruct((HL, B, B), BF16),) * 4
        + (jax.ShapeDtypeStruct((HL * B, B), BF16),) * 2,
        in_specs=[full] * 8,
        out_specs=(full,) * 6,
        scratch_shapes=[
            pltpu.VMEM((nz, HL, 5, 2, B, B), BF16),
            pltpu.VMEM((nz, HL, 4, B, B), F32),
            pltpu.VMEM((nz, HL, 4, B, B), F32),
            per_head,
            per_head,
            per_head,
            per_head,
            pltpu.VMEM((2, HL, B, B), F32),
            per_head,
            per_head,
            per_head,
            per_head,
            pltpu.VMEM((HL * B, B), BF16),
            pltpu.VMEM((NY, nz, 2 * HL, B), F32),
            pltpu.VMEM((16, B), F32),
            pltpu.VMEM((NY, nz, 16, B), F32),
            pltpu.VMEM((2, nh, 8, B), F32),
            pltpu.VMEM((2, 8, B), F32),
            sem((nz, HL)),
            sem((nz, HL)),
            sem((nz, 2)),
            sem((nz, 2)),
            sem((nz, HL)),
            sem((nz, HL)),
            sem((nz, HL, 3)),
            sem((nz, HL, 2)),
            sem((5, max(nz, NY))),
            sem((5, max(nz, NY))),
            sem((4, nh)),
        ]
        + scan_scratch(nz) * 2,
        compiler_params=pltpu.CompilerParams(
            collective_id=0, has_side_effects=True, vmem_limit_bytes=56 << 20
        ),
    )(own.reshape(HL, 2, 2, B, B), lin, decay, gain, state, fin, bias, mask)


def last_kernel(lin, dec, state_in, cot, rev, dq_in, dk_in, dv_in, dq_o, dk_o, dv_o, sq_o, sk_o, sv_o, tmp):
    run = running_of(dec[...])
    trail = jnp.exp(run[:, B - 1 : B] - run)
    keep = iota(0) <= iota(1)

    def put(ref, value):
        for h in range(HL):
            tmp[pl.ds(h, B, stride=HL), :] = value(h)
        ref[...] = tmp[...].astype(BF16)

    def dq(h):
        row = run[h : h + 1]
        col = col_of(row)
        pair = (mm_t(cot[h], lin[h, 2]) * within_of(row, col)).astype(BF16)
        return mm(pair, lin[h, 1]) + jnp.exp(col) * mm_t(cot[h], state_in[pl.ds(h * B, B), :])

    def within_t(h):
        row = run[h : h + 1]
        return jnp.where(keep, jnp.exp(jnp.where(keep, row - col_of(row), 0.0)), 0.0)

    def dk(h):
        pair = (mm_t(lin[h, 2], cot[h]) * within_t(h)).astype(BF16)
        return mm(pair, lin[h, 0]) + col_of(trail[h : h + 1]) * mm_t(lin[h, 2], rev[pl.ds(h * B, B), :])

    def dv(h):
        pair = (mm_t(lin[h, 1], lin[h, 0]) * within_t(h)).astype(BF16)
        return mm(pair, cot[h]) + col_of(trail[h : h + 1]) * mm(lin[h, 1], rev[pl.ds(h * B, B), :])

    put(dq_o, dq)
    put(dk_o, dk)
    put(dv_o, dv)
    put(sq_o, lambda h: dq_in[h].astype(F32))
    put(sk_o, lambda h: dk_in[h].astype(F32))
    put(sv_o, lambda h: dv_in[h].astype(F32))


def last(lin, dec, state_in, cot, rev, dq, dk, dv):
    full = pl.BlockSpec(memory_space=pltpu.VMEM)
    return pl.pallas_call(
        last_kernel,
        out_shape=(jax.ShapeDtypeStruct((HL * B, B), BF16),) * 6,
        in_specs=[full] * 8,
        out_specs=(full,) * 6,
        scratch_shapes=[pltpu.VMEM((HL * B, B), F32)],
    )(lin, dec, state_in, cot, rev, dq, dk, dv)


def local(nz, nh, lin_q, lin_k, lin_v, decay, gain, soft_q, soft_k, soft_v, out_grad, lists, counts):
    flat = [a.reshape(B * HL, B) for a in (lin_q, lin_k, lin_v, soft_q, soft_k, soft_v, out_grad)]
    own, lin, state, fin, bias, mask = prep(nz, lists, counts, flat, decay)
    dq, dk, dv, cot, rev, state_in = fused(nz, nh, own, lin, decay, gain, state, fin, bias, mask)
    grads = last(lin, decay, state_in, cot, rev, dq, dk, dv)
    return tuple(a.reshape(B, HL, B) for a in grads)


def solution(mesh):
    nz = mesh.shape["ctx"] // NY
    tokens = P("ctx", "head", None)
    in_specs = (
        (tokens,) * 3 + (P("head", "ctx"), P("head", None)) + (tokens,) * 4 + (P("ctx", None), P("ctx"))
    )
    return jax.shard_map(
        functools.partial(local, nz, mesh.shape["head"]),
        mesh=mesh,
        in_specs=in_specs,
        out_specs=(tokens,) * 6,
        check_vma=False,
    )
```

time: 197 us -> 143 us (0.73); the launches traced: 194 us -> 142 us
  Pallas kernels: 192 us -> 141 us
    pallas_call x4 -> x2, Pallas kernels: 189 us -> 137 us  [the longest x1 134 us: fused(): pl.pallas_call(functools.partial(fused_kernel, nz, nh), out_shape=(jax.Sh...]
where the time goes in v2:
time: 143 us; the launch traced here: 142 us
  Pallas kernels  141 us (99%)
    pallas_call x1, Pallas kernels, fused(): pl.pallas_call(functools.partial(fused_kernel, nz, nh), out_shape=(jax.Sh...  134 us
    pallas_call x1, Pallas kernels, last(): pl.pallas_call(last_kernel, out_shape=(jax.ShapeDtypeStruct((HL * B, B),...  3.54 us

profile of v2, /device:TPU:32, one launch (start us, length us, event | category | flops | bytes accessed | tf_op | source)
XLA Modules:
  0.0 142.1 jit_solution(7245389901703309848)
XLA Ops:
  1.3 2.8 %shard_map.154 = (bf16[4,4,128,128]{3,2,1,0:T(8,128)(2,1)}, bf16[4,3,128,128]{3,2,1,0:T(8,128)(2,1)}, bf16[512,128]{1,0:T(8,128)(2,1)}, f32[8,128]{1,0:T(8,128)}...) custom-call(s32[1,16]{1,0:T(1,128)} %lists.1, s32[1]{0:T(128)S(6)} %copy.17.count, bf16[512,128]{1,0:T(8,128)(2,1)} %bitcast.15, ...), custom_call_target="tpu_custom_call" | custom-call | tf_op jit(solution)/shard_map/pallas_call | solution.py:130
  4.1 134.4 %shard_map.155 = (bf16[4,128,128]{2,1,0:T(8,128)(2,1)}, bf16[4,128,128]{2,1,0:T(8,128)(2,1)}, bf16[4,128,128]{2,1,0:T(8,128)(2,1)}, bf16[4,128,128]{2,1,0:T(8,12...) custom-call(bf16[4,2,2,128,128]{4,3,2,1,0:T(8,128)(2,1)} %bitcast.14, ...), custom_call_target="tpu_custom_call" | custom-call | tf_op jit(solution)/shard_map/pallas_call | solution.py:667
  138.5 3.5 %shard_map.156 = (bf16[512,128]{1,0:T(8,128)(2,1)}, bf16[512,128]{1,0:T(8,128)(2,1)}, bf16[512,128]{1,0:T(8,128)(2,1)}, bf16[512,128]{1,0:T(8,128)(2,1)}, bf16[5...) custom-call(bf16[4,3,128,128]{3,2,1,0:T(8,128)(2,1)} %get-tuple-element.24.lin, f32[4,128]{1,0:T(4,128)} %dec.5, ...), custom_call_target="tpu_custom_call" | custom-call | tf_op jit(solution)/shard_map/pallas_call | solution.py:749

commit v3 on v2

v3 whole, which is shorter than its diff:
```python
import functools

import jax
import jax.numpy as jnp
from jax import lax
from jax.experimental import pallas as pl
from jax.experimental.pallas import tpu as pltpu
from jax.sharding import PartitionSpec as P

NY = 4
HL = 4
B = 128
NSEL = 16
FR = 48
EPS = 1e-05
SCALE = 128 ** (-0.5)
NEG = -1e30
BIG = 1e30
F32 = jnp.float32
BF16 = jnp.bfloat16
MESH = pl.DeviceIdType.MESH
HIGH = lax.Precision.HIGHEST


def mm(a, b):
    return lax.dot_general(a, b, (((1,), (0,)), ((), ())), preferred_element_type=F32)


def mm_t(a, b):
    return lax.dot_general(a, b, (((1,), (1,)), ((), ())), preferred_element_type=F32)


def t_mm(a, b):
    return lax.dot_general(a, b, (((0,), (0,)), ((), ())), preferred_element_type=F32)


def iota(dim):
    return lax.broadcasted_iota(jnp.int32, (B, B), dim)


def col_of(row):
    return jnp.transpose(jnp.broadcast_to(row, (B, B)))


def row_of(col):
    return jnp.transpose(jnp.broadcast_to(col, (B, B)))[0:1]


def running_of(decay):
    upper = (iota(0) <= iota(1)).astype(F32)
    return lax.dot_general(
        decay, upper, (((1,), (0,)), ((), ())), precision=HIGH, preferred_element_type=F32
    )


def within_of(row, col):
    keep = iota(0) >= iota(1)
    return jnp.where(keep, jnp.exp(jnp.where(keep, col - row, 0.0)), 0.0)


def slot_of(r, y):
    return jnp.where(lax.rem(y + NY - 1, NY) == r, 0, jnp.where(lax.rem(y + 1, NY) == r, 1, 2))


def place(nz):
    own = lax.axis_index("ctx")
    return own // nz, lax.rem(own, nz)


def start_remote(src, dst, send, recv, ctx, head):
    pltpu.make_async_remote_copy(
        src_ref=src, dst_ref=dst, send_sem=send, recv_sem=recv, device_id=(ctx, head), device_id_type=MESH
    ).start()


def wait_recv(ref, recv, ctx, head):
    pltpu.make_async_remote_copy(
        src_ref=ref, dst_ref=ref, send_sem=recv, recv_sem=recv, device_id=(ctx, head), device_id_type=MESH
    ).wait_recv()


def wait_send(ref, send, ctx, head):
    pltpu.make_async_remote_copy(
        src_ref=ref, dst_ref=ref, send_sem=send, recv_sem=send, device_id=(ctx, head), device_id_type=MESH
    ).wait_send()


def scan_scratch(nz):
    rs = HL * B // nz
    return [
        pltpu.VMEM((nz, rs, B), BF16),
        pltpu.VMEM((nz, rs, B), F32),
        pltpu.VMEM((NY, rs, B), F32),
        pltpu.VMEM((rs, B), F32),
        pltpu.VMEM((nz, rs, B), BF16),
        pltpu.SemaphoreType.DMA((6, nz)),
        pltpu.SemaphoreType.DMA((2,)),
    ]


def scan_start(nz, head, local, bufs):
    zbuf, sems, lsem = bufs[0], bufs[5], bufs[6]
    rs = HL * B // nz
    y, z = place(nz)
    for d in range(1, nz):
        zz = lax.rem(z + d, nz)
        start_remote(
            local.at[pl.ds(zz * rs, rs)], zbuf.at[z], sems.at[0, zz], sems.at[1, z], y * nz + zz, head
        )
    pltpu.make_async_copy(local.at[pl.ds(z * rs, rs)], zbuf.at[z], lsem.at[0]).start()


def scan_rows(nz, head, local, fin, bufs, reverse):
    zbuf, ebuf, tbuf, tsrc, _, sems, lsem = bufs
    rs = HL * B // nz
    y, z = place(nz)
    own = y * nz + z
    hz = z * rs // B
    pltpu.make_async_copy(local.at[pl.ds(z * rs, rs)], zbuf.at[z], lsem.at[0]).wait()
    for d in range(1, nz):
        zz = lax.rem(z + d, nz)
        wait_recv(zbuf.at[zz], sems.at[1, zz], own, head)

    total = jnp.zeros((rs, B), F32)
    for lap in range(nz):
        m = nz - 1 - lap if reverse else lap
        ebuf[m] = total
        total = total * jnp.exp(fin[y, m, pl.ds(hz, 1), :]) + zbuf[m].astype(F32)
    tsrc[...] = total
    for d in range(1, NY):
        yy = lax.rem(y + d, NY)
        start_remote(tsrc, tbuf.at[y], sems.at[2, yy], sems.at[3, y], yy * nz + z, head)
    for d in range(1, nz):
        zz = lax.rem(z + d, nz)
        wait_send(zbuf.at[0], sems.at[0, zz], own, head)


def scan_spread(nz, head, fin, out, bufs, reverse):
    _, ebuf, tbuf, tsrc, sbuf, sems, lsem = bufs
    rs = HL * B // nz
    y, z = place(nz)
    own = y * nz + z
    hz = z * rs // B
    for d in range(1, NY):
        yy = lax.rem(y + d, NY)
        wait_recv(tbuf.at[yy], sems.at[3, yy], own, head)
        wait_send(tsrc, sems.at[2, yy], own, head)
    carry = jnp.zeros((rs, B), F32)
    for lap in range(NY):
        r = NY - 1 - lap if reverse else lap
        use = (r > y) if reverse else (r < y)
        span = jnp.zeros((1, B), F32)
        for m in range(nz):
            span = span + fin[r, m, pl.ds(hz, 1), :]
        carry = jnp.where(use, carry * jnp.exp(span) + tbuf[r], carry)
    for lap in range(nz):
        m = nz - 1 - lap if reverse else lap
        sbuf[m] = (ebuf[m] + carry).astype(BF16)
        carry = carry * jnp.exp(fin[y, m, pl.ds(hz, 1), :])
    for d in range(1, nz):
        zz = lax.rem(z + d, nz)
        start_remote(
            sbuf.at[zz], out.at[pl.ds(z * rs, rs)], sems.at[4, zz], sems.at[5, z], y * nz + zz, head
        )
    pltpu.make_async_copy(sbuf.at[z], out.at[pl.ds(z * rs, rs)], lsem.at[1]).start()


def scan_finish(nz, head, out, bufs):
    sbuf, sems, lsem = bufs[4], bufs[5], bufs[6]
    rs = HL * B // nz
    y, z = place(nz)
    own = y * nz + z
    for d in range(1, nz):
        zz = lax.rem(z + d, nz)
        wait_recv(out.at[pl.ds(zz * rs, rs)], sems.at[5, zz], own, head)
        wait_send(sbuf.at[zz], sems.at[4, zz], own, head)
    pltpu.make_async_copy(sbuf.at[z], out.at[pl.ds(z * rs, rs)], lsem.at[1]).wait()


def small_start(nz, head, src, dst, sems):
    y, z = place(nz)
    for d in range(1, nz):
        zz = lax.rem(z + d, nz)
        start_remote(src, dst.at[y, z], sems.at[0, zz], sems.at[1, z], y * nz + zz, head)
    pltpu.make_async_copy(src, dst.at[y, z], sems.at[2, 0]).start()


def small_rows(nz, head, src, dst, sems):
    y, z = place(nz)
    own = y * nz + z
    for d in range(1, nz):
        zz = lax.rem(z + d, nz)
        wait_recv(dst.at[y, zz], sems.at[1, zz], own, head)
    pltpu.make_async_copy(src, dst.at[y, z], sems.at[2, 0]).wait()
    for d in range(1, NY):
        yy = lax.rem(y + d, NY)
        start_remote(dst.at[y], dst.at[y], sems.at[3, yy], sems.at[4, y], yy * nz + z, head)


def small_finish(nz, head, src, dst, sems):
    y, z = place(nz)
    own = y * nz + z
    for d in range(1, NY):
        yy = lax.rem(y + d, NY)
        wait_recv(dst.at[yy], sems.at[4, yy], own, head)


def small_drain(nz, head, src, dst, sems):
    y, z = place(nz)
    own = y * nz + z
    for d in range(1, nz):
        zz = lax.rem(z + d, nz)
        wait_send(src, sems.at[0, zz], own, head)
    for d in range(1, NY):
        yy = lax.rem(y + d, NY)
        wait_send(dst.at[y], sems.at[3, yy], own, head)


def greet(nz, head, nh):
    y, z = place(nz)
    barrier = pltpu.get_barrier_semaphore()
    for d in range(1, nz):
        pl.semaphore_signal(
            barrier, inc=1, device_id=(y * nz + lax.rem(z + d, nz), head), device_id_type=MESH
        )
    for d in range(1, NY):
        pl.semaphore_signal(
            barrier, inc=1, device_id=(lax.rem(y + d, NY) * nz + z, head), device_id_type=MESH
        )
    for d in range(1, nh):
        pl.semaphore_signal(
            barrier, inc=1, device_id=(y * nz + z, lax.rem(head + d, nh)), device_id_type=MESH
        )


def greeted(nz, nh):
    pl.semaphore_wait(pltpu.get_barrier_semaphore(), nz - 1 + NY - 1 + nh - 1)


def fused_kernel(
    nz,
    nh,
    lists,
    count,
    lq,
    lk,
    lv,
    sq,
    sk,
    sv,
    og,
    dec,
    gain,
    dq_out,
    dk_out,
    dv_out,
    lin_dq,
    part_dk,
    part_dv,
    rev_out,
    lin,
    own,
    pairs,
    a1,
    a2,
    mx,
    ls,
    acc,
    dkq,
    lcol,
    dcol,
    lo,
    cot,
    bias,
    state,
    state_in,
    fin_own,
    fin,
    lse_own,
    lse_all,
    del_own,
    del_all,
    hbuf,
    hsrc,
    tmp,
    ring_s,
    ring_r,
    bun_s,
    bun_r,
    up_s,
    dn_s,
    col_r,
    rel_s,
    fsem,
    lsem,
    dsem,
    hsem,
    *scans,
):
    fwd, bwd = scans[: len(scans) // 2], scans[len(scans) // 2 :]
    head = lax.axis_index("head")
    y, z = place(nz)
    me = y * nz + z
    n = NY * nz
    right, left = y * nz + lax.rem(z + 1, nz), y * nz + lax.rem(z + nz - 1, nz)
    above, below = lax.rem(y + 1, NY) * nz + z, lax.rem(y + NY - 1, NY) * nz + z
    part_up = jnp.where(y < NY - 1, 0, 1)
    part_dn = jnp.where(y > 0, 1, 0)
    inner_row = (y == 1) | (y == 2)
    greet(nz, head, nh)

    def heads(ref, store):
        tmp[...] = ref[...].astype(F32)
        for h in range(HL):
            store(h, tmp[pl.ds(h, B, stride=HL), :].astype(BF16))

    def own_at(t, a):
        def store(h, value):
            own[h, t, a] = value

        return store

    def lin_at(i):
        def store(h, value):
            lin[h, i] = value

        return store

    heads(sk, own_at(0, 0))
    heads(sq, own_at(1, 0))
    heads(sv, own_at(0, 1))
    heads(og, own_at(1, 1))
    greeted(nz, nh)

    def at(s, h):
        return lax.rem(z + nz - s, nz) if h % 2 == 0 else lax.rem(z + s, nz)

    def to_next(h):
        return right if h % 2 == 0 else left

    def ring(a, zz, h):
        return pairs.at[zz, h, pl.ds(3, 2), a]

    def ring_on(a, zz, h, src=None):
        start_remote(
            ring(a, zz, h) if src is None else src,
            ring(a, zz, h),
            ring_s.at[a, zz, h],
            ring_r.at[a, zz, h],
            to_next(h),
            head,
        )

    def bundle(a, zz, h):
        return pairs.at[zz, h, pl.ds(0, 3), a, pl.ds(FR, B - FR)]

    def bundle_on(a, zz, h):
        ref = bundle(a, zz, h)
        start_remote(ref, ref, bun_s.at[a, zz, h - 2], bun_r.at[a, zz, h - 2], to_next(h), head)

    def cell(a, zz, h, slot, rows):
        return pairs.at[zz, h, slot, a, pl.ds(0, rows)]

    def column_on(a, zz, h, up, dn, rows):
        start_remote(up, cell(a, zz, h, 0, rows), up_s.at[a, zz, h], col_r.at[a, zz, h, 0], above, head)
        start_remote(dn, cell(a, zz, h, 1, rows), dn_s.at[a, zz, h], col_r.at[a, zz, h, 1], below, head)

    def rows_of(h):
        return B if h < 2 else FR

    def begin(a):
        def column_own(h):
            column_on(a, z, h, own.at[h, part_up, a], own.at[h, part_dn, a], B)

        for h in (0, 1):
            ring_on(a, z, h, own.at[h, pl.ds(0, 2), a])
        for h in (2, 3):
            column_own(h)
        for h in (2, 3):
            ring_on(a, z, h, own.at[h, pl.ds(0, 2), a])
        for h in (0, 1):
            column_own(h)

    def relay(a, zz, h, rows):
        for k in (0, 1):
            wait_recv(cell(a, zz, h, k, rows), col_r.at[a, zz, h, k], me, head)

        @pl.when(inner_row)
        def _():
            for k, to in ((0, above), (1, below)):
                start_remote(
                    cell(a, zz, h, k, rows),
                    cell(a, zz, h, 2, rows),
                    rel_s.at[a, zz, h, k],
                    col_r.at[a, zz, h, 2],
                    to,
                    head,
                )

    def opposite(a, zz, h, rows):
        wait_recv(cell(a, zz, h, 2, rows), col_r.at[a, zz, h, 2], me, head)

    def lap(a, s, first=False, second=False, last=False):
        for h in range(HL):
            zz = at(s, h)
            wait_recv(ring(a, zz, h), ring_r.at[a, zz, h], me, head)
            if not last:
                ring_on(a, zz, h)
            rows = rows_of(h)
            column_on(a, zz, h, cell(a, zz, h, 3 + part_up, rows), cell(a, zz, h, 3 + part_dn, rows), rows)
        if first:
            for h in (2, 3):
                relay(a, z, h, B)
            for h in (2, 3):
                opposite(a, z, h, B)
                bundle_on(a, z, h)
            for h in (0, 1):
                relay(a, z, h, B)
        else:
            for h in range(HL):
                relay(a, at(s - 1, h), h, rows_of(h))
        for h in (2, 3):
            zz = at(s, h)
            wait_recv(bundle(a, zz, h), bun_r.at[a, zz, h - 2], me, head)
            if not last:
                bundle_on(a, zz, h)
        if second:
            for h in (0, 1):
                opposite(a, z, h, B)
        elif not first:
            for h in range(HL):
                opposite(a, at(s - 2, h), h, rows_of(h))

    lane = lax.broadcasted_iota(jnp.int32, (1, B), 1)
    causal = iota(0) >= iota(1)

    def kinds(zz, with_row):
        found = []
        for k, off in ((0, NY - 1), (1, 1), (2, 2)):
            r = lax.rem(y + off, NY)
            found.append((k, k, jnp.where(r < y, 1, 0), r))
        if with_row:
            t = jnp.where(zz < z, 1, 0)
            found.append((3, 4 - t, t, y))
        return found

    def score(zz, h, with_row):
        scores = []
        for k, slot, t, _ in kinds(zz, with_row):
            s = mm_t(own[h, t, 0], pairs[zz, h, slot, 0]) * SCALE
            a1[zz, h, k] = s
            scores.append(s + bias[k, pl.ds(zz, 1), :])
        top = functools.reduce(jnp.maximum, scores)
        m = jnp.maximum(mx[h], jnp.broadcast_to(jnp.max(top, axis=1, keepdims=True), (B, B)))
        total = ls[h] * jnp.exp(mx[h] - m)
        for s in scores:
            total = total + jnp.exp(s - m)
        mx[h] = m
        ls[h] = total

    def weigh(zz, h, with_row):
        for k, slot, t, r in kinds(zz, with_row):
            here = jnp.sum(
                jnp.where(lane == me, fin[r, zz, HL : HL + 1, :], 0.0), axis=1, keepdims=True
            )
            theirs = jnp.where(here > 0.5, lse_all[r, zz, h : h + 1, :], BIG)
            lse = jnp.where(t == 1, lcol[h] - bias[k, pl.ds(zz, 1), :], theirs)
            v = pairs[zz, h, slot, 1]
            p = jnp.exp(a1[zz, h, k] - lse)
            a1[zz, h, k] = p
            a2[zz, h, k] = mm_t(own[h, t, 1], v)
            acc[t, h] = acc[t, h] + mm(p.astype(BF16), v)

    begin(0)

    for h in range(HL):
        s = jnp.where(causal, mm_t(own[h, 1, 0], own[h, 0, 0]) * SCALE, NEG)
        m = jnp.broadcast_to(jnp.max(s, axis=1, keepdims=True), (B, B))
        mx[h] = m
        ls[h] = jnp.exp(s - m)
    column = lax.broadcasted_iota(jnp.int32, (nz, B), 0)
    named = jnp.zeros((1, B), F32)
    for e in range(NSEL):
        named = jnp.where((lane == lists[0, e]) & (e < count[0]), 1.0, named)
    for k, off in ((0, NY - 1), (1, 1), (2, 2), (3, 0)):
        block = lax.rem(y + off, NY) * nz + column
        b = jnp.full((nz, B), NEG, F32)
        for e in range(NSEL):
            b = jnp.where((block == lists[0, e]) & (e < count[0]), 0.0, b)
        bias[k] = b
    heads(lk, lin_at(1))
    heads(lv, lin_at(2))
    heads(lq, lin_at(0))
    run = running_of(dec[...])
    finish = run[:, B - 1 : B]
    fin_own[...] = jnp.concatenate(
        [jnp.broadcast_to(finish, (HL, B)), named, jnp.zeros((HL - 1, B), F32)], axis=0
    )
    trailing = jnp.exp(finish - run)
    for h in range(HL):
        k = lin[h, 1].astype(F32) * col_of(trailing[h : h + 1])
        state[pl.ds(h * B, B), :] = t_mm(k.astype(BF16), lin[h, 2]).astype(BF16)

    lap(0, 1, first=True)
    small_start(nz, head, fin_own, fin, fsem)
    scan_start(nz, head, state, fwd)
    lap(0, 2, second=True)
    for h in range(HL):
        score(z, h, False)
    small_rows(nz, head, fin_own, fin, fsem)
    scan_rows(nz, head, state, fin, fwd, False)

    @pl.loop(3, nz - 1)
    def _(s):
        lap(0, s)
        for h in range(HL):
            score(at(s - 2, h), h, True)

    begin(1)
    lap(0, nz - 1, last=True)
    for h in range(HL):
        score(at(nz - 3, h), h, True)
    for h in range(HL):
        relay(0, at(nz - 1, h), h, rows_of(h))
    lap(1, 1, first=True)
    for s in (nz - 2, nz - 1):
        for h in range(HL):
            opposite(0, at(s, h), h, rows_of(h))
        for h in range(HL):
            score(at(s, h), h, True)
    lse_own[...] = jnp.zeros_like(lse_own)
    for h in range(HL):
        lse = mx[h] + jnp.log(jnp.sum(ls[h], axis=1, keepdims=True))
        lcol[h] = lse
        lse_own[h : h + 1, :] = jnp.transpose(lse)[0:1]
    small_start(nz, head, lse_own, lse_all, lsem)
    small_finish(nz, head, fin_own, fin, fsem)
    scan_spread(nz, head, fin, state_in, fwd, False)
    lap(1, 2, second=True)
    small_rows(nz, head, lse_own, lse_all, lsem)
    for h in range(HL):
        p = jnp.where(causal, jnp.exp(mm_t(own[h, 1, 0], own[h, 0, 0]) * SCALE - lcol[h]), 0.0)
        dp = mm_t(own[h, 1, 1], own[h, 0, 1])
        a1[z, h, 3] = p
        a2[z, h, 3] = dp
        low = p.astype(BF16)
        acc[1, h] = mm(low, own[h, 0, 1])
        acc[0, h] = t_mm(low, own[h, 1, 1])
    lap(1, 3)
    small_finish(nz, head, lse_own, lse_all, lsem)
    for h in range(HL):
        weigh(z, h, False)
    for h in range(HL):
        weigh(at(1, h), h, True)

    def heads_start(k):
        for d in range(1, nh):
            hh = lax.rem(head + d, nh)
            start_remote(hsrc.at[k], hbuf.at[k, head], hsem.at[2 * k, hh], hsem.at[2 * k + 1, head], me, hh)

    def heads_total(k):
        total = hsrc[k]
        for d in range(1, nh):
            hh = lax.rem(head + d, nh)
            wait_recv(hbuf.at[k, hh], hsem.at[2 * k + 1, hh], me, head)
            total = total + hbuf[k, hh]
            wait_send(hsrc.at[k], hsem.at[2 * k, hh], me, head)
        return total[0:1]

    if nz > 4:
        lap(1, 4)
        for h in range(HL):
            weigh(at(2, h), h, True)

    scan_finish(nz, head, state_in, fwd)
    squares = jnp.zeros((B, 1), F32)
    for h in range(HL):
        row = run[h : h + 1]
        col = col_of(row)
        w = (mm_t(lin[h, 0], lin[h, 1]) * within_of(row, col)).astype(BF16)
        o = mm(w, lin[h, 2]) + jnp.exp(col) * mm(lin[h, 0], state_in[pl.ds(h * B, B), :])
        lo[h] = o
        squares = squares + jnp.sum(o * o, axis=1, keepdims=True)
    hsrc[0] = jnp.broadcast_to(row_of(squares), (8, B))
    heads_start(0)

    if nz > 4:

        @pl.loop(5, nz - 1)
        def _(s):
            lap(1, s)
            for h in range(HL):
                weigh(at(s - 2, h), h, True)

        lap(1, nz - 1, last=True)
        for h in range(HL):
            weigh(at(nz - 3, h), h, True)
    for h in range(HL):
        relay(1, at(nz - 1, h), h, rows_of(h))
    for s in (nz - 2, nz - 1):
        for h in range(HL):
            opposite(1, at(s, h), h, rows_of(h))
        for h in range(HL):
            weigh(at(s, h), h, True)

    partial = jnp.zeros((B, 1), F32)
    for h in range(HL):
        c = (acc[0, h] + own[h, 1, 1].astype(F32)) * gain[h : h + 1, :]
        cot[h] = c
        partial = partial + jnp.sum(c * lo[h], axis=1, keepdims=True)
    hsrc[1] = jnp.broadcast_to(row_of(partial), (8, B))
    heads_start(1)

    del_own[...] = jnp.zeros_like(del_own)
    for h in range(HL):
        dv_out[h] = acc[0, h].astype(BF16)
        delta = jnp.sum(own[h, 1, 1].astype(F32) * acc[1, h], axis=1, keepdims=True)
        delta = jnp.broadcast_to(delta, (B, B))
        dcol[h] = delta
        del_own[h : h + 1, :] = jnp.transpose(delta)[0:1]
    small_start(nz, head, del_own, del_all, dsem)
    for h in range(HL):
        ds = (a1[z, h, 3] * (a2[z, h, 3] - dcol[h])).astype(BF16)
        dkq[1, h] = mm(ds, own[h, 0, 0])
        dkq[0, h] = t_mm(ds, own[h, 1, 0])

    def key_grads(lo_i, hi_i):
        @pl.loop(lo_i, jnp.minimum(hi_i, me))
        def _(i):
            r, zz = i // nz, lax.rem(i, nz)
            k = jnp.where(r == y, 3, slot_of(r, y))
            for h in range(HL):
                ds = (a1[zz, h, k] * (a2[zz, h, k] - dcol[h])).astype(BF16)
                dkq[1, h] = dkq[1, h] + mm(ds, pairs[zz, h, k, 0])

    def query_grads(lo_i, hi_i):
        @pl.loop(jnp.maximum(lo_i, me + 1), hi_i)
        def _(i):
            r, zz = i // nz, lax.rem(i, nz)
            k = jnp.where(r == y, 3, slot_of(r, y))
            slot = jnp.where(r == y, 4, k)
            for h in range(HL):
                ds = (a1[zz, h, k] * (a2[zz, h, k] - del_all[r, zz, h : h + 1, :])).astype(BF16)
                dkq[0, h] = dkq[0, h] + mm(ds, pairs[zz, h, slot, 0])

    width = HL * nh * B
    root = jnp.sqrt(heads_total(0) / width + EPS)
    inner = heads_total(1)
    factor = col_of(inner / (width * root * root * root))
    inv = col_of(1.0 / root)
    leading = jnp.exp(run)
    for h in range(HL):
        lc = cot[h] * inv - lo[h] * factor
        cot[h] = lc
        q = (lin[h, 0].astype(F32) * col_of(leading[h : h + 1])).astype(BF16)
        state[pl.ds(h * B, B), :] = t_mm(q, lc.astype(BF16)).astype(BF16)
    scan_start(nz, head, state, bwd)
    key_grads(0, n // 2)
    small_rows(nz, head, del_own, del_all, dsem)
    scan_rows(nz, head, state, fin, bwd, True)
    for h in range(HL):
        row = run[h : h + 1]
        col = col_of(row)
        within = within_of(row, col)
        c = cot[h].astype(BF16)
        pair = (mm_t(c, lin[h, 2]) * within).astype(BF16)
        w = (mm_t(lin[h, 0], lin[h, 1]) * within).astype(BF16)
        o = mm(pair, lin[h, 1]) + jnp.exp(col) * mm_t(c, state_in[pl.ds(h * B, B), :])
        lin_dq[h] = o.astype(BF16)
        part_dk[h] = t_mm(pair, lin[h, 0])
        part_dv[h] = t_mm(w, c)
    small_finish(nz, head, del_own, del_all, dsem)
    scan_spread(nz, head, fin, rev_out, bwd, True)
    key_grads(n // 2, n)
    query_grads(0, n)
    for h in range(HL):
        dk_out[h] = (dkq[0, h] * SCALE).astype(BF16)
        dq_out[h] = (dkq[1, h] * SCALE).astype(BF16)
    scan_finish(nz, head, rev_out, bwd)

    small_drain(nz, head, fin_own, fin, fsem)
    small_drain(nz, head, lse_own, lse_all, lsem)
    small_drain(nz, head, del_own, del_all, dsem)

    for a in range(2):

        def column_left(zz, h, rows):
            wait_send(cell(a, zz, h, 0, rows), up_s.at[a, zz, h], me, head)
            wait_send(cell(a, zz, h, 1, rows), dn_s.at[a, zz, h], me, head)

            @pl.when(inner_row)
            def _():
                for k in (0, 1):
                    wait_send(cell(a, zz, h, k, rows), rel_s.at[a, zz, h, k], me, head)

        for h in range(HL):
            column_left(z, h, B)

        @pl.loop(0, nz - 1)
        def _(s):
            for h in range(HL):
                zz = at(s, h)
                wait_send(ring(a, zz, h), ring_s.at[a, zz, h], me, head)
                if h >= 2:
                    wait_send(bundle(a, zz, h), bun_s.at[a, zz, h - 2], me, head)
                column_left(at(s + 1, h), h, rows_of(h))


def fused(nz, nh, lists, counts, arrays, decay, gain):
    full = pl.BlockSpec(memory_space=pltpu.VMEM)
    smem = pl.BlockSpec(memory_space=pltpu.SMEM)
    sem = pltpu.SemaphoreType.DMA
    per_head = pltpu.VMEM((HL, B, B), F32)
    small = pltpu.VMEM((2 * HL, B), F32)
    small_all = pltpu.VMEM((NY, nz, 2 * HL, B), F32)
    low = jax.ShapeDtypeStruct((HL, B, B), BF16)
    wide = jax.ShapeDtypeStruct((HL, B, B), F32)
    return pl.pallas_call(
        functools.partial(fused_kernel, nz, nh),
        out_shape=(low,) * 4
        + (wide,) * 2
        + (jax.ShapeDtypeStruct((HL * B, B), BF16), jax.ShapeDtypeStruct((HL, 3, B, B), BF16)),
        in_specs=[smem, smem] + [full] * 9,
        out_specs=(full,) * 8,
        scratch_shapes=[
            pltpu.VMEM((HL, 2, 2, B, B), BF16),
            pltpu.VMEM((nz, HL, 5, 2, B, B), BF16),
            pltpu.VMEM((nz, HL, 4, B, B), F32),
            pltpu.VMEM((nz, HL, 4, B, B), F32),
            per_head,
            per_head,
            pltpu.VMEM((2, HL, B, B), F32),
            pltpu.VMEM((2, HL, B, B), F32),
            per_head,
            per_head,
            per_head,
            per_head,
            pltpu.VMEM((4, nz, B), F32),
            pltpu.VMEM((HL * B, B), BF16),
            pltpu.VMEM((HL * B, B), BF16),
            small,
            small_all,
            small,
            small_all,
            small,
            small_all,
            pltpu.VMEM((2, nh, 8, B), F32),
            pltpu.VMEM((2, 8, B), F32),
            pltpu.VMEM((HL * B, B), F32),
            sem((2, nz, HL)),
            sem((2, nz, HL)),
            sem((2, nz, 2)),
            sem((2, nz, 2)),
            sem((2, nz, HL)),
            sem((2, nz, HL)),
            sem((2, nz, HL, 3)),
            sem((2, nz, HL, 2)),
            sem((5, max(nz, NY))),
            sem((5, max(nz, NY))),
            sem((5, max(nz, NY))),
            sem((4, nh)),
        ]
        + scan_scratch(nz) * 2,
        compiler_params=pltpu.CompilerParams(
            collective_id=0, has_side_effects=True, vmem_limit_bytes=56 << 20
        ),
    )(lists, counts, *arrays, decay, gain)


def last_kernel(lin, dec, rev, dq, dk, dv, lq, pdk, pdv, o_lq, o_lk, o_lv, o_q, o_k, o_v, tmp):
    run = running_of(dec[...])
    trail = jnp.exp(run[:, B - 1 : B] - run)

    def put(ref, value):
        for h in range(HL):
            tmp[pl.ds(h, B, stride=HL), :] = value(h)
        ref[...] = tmp[...].astype(BF16)

    def lin_dk(h):
        return pdk[h] + col_of(trail[h : h + 1]) * mm_t(lin[h, 2], rev[pl.ds(h * B, B), :])

    def lin_dv(h):
        return pdv[h] + col_of(trail[h : h + 1]) * mm(lin[h, 1], rev[pl.ds(h * B, B), :])

    put(o_lq, lambda h: lq[h].astype(F32))
    put(o_lk, lin_dk)
    put(o_lv, lin_dv)
    put(o_q, lambda h: dq[h].astype(F32))
    put(o_k, lambda h: dk[h].astype(F32))
    put(o_v, lambda h: dv[h].astype(F32))


def last(lin, decay, rev, *parts):
    full = pl.BlockSpec(memory_space=pltpu.VMEM)
    return pl.pallas_call(
        last_kernel,
        out_shape=(jax.ShapeDtypeStruct((HL * B, B), BF16),) * 6,
        in_specs=[full] * 9,
        out_specs=(full,) * 6,
        scratch_shapes=[pltpu.VMEM((HL * B, B), F32)],
    )(lin, decay, rev, *parts)


def local(nz, nh, lin_q, lin_k, lin_v, decay, gain, soft_q, soft_k, soft_v, out_grad, lists, counts):
    flat = [a.reshape(B * HL, B) for a in (lin_q, lin_k, lin_v, soft_q, soft_k, soft_v, out_grad)]
    dq, dk, dv, lin_dq, part_dk, part_dv, rev, lin = fused(nz, nh, lists, counts, flat, decay, gain)
    grads = last(lin, decay, rev, dq, dk, dv, lin_dq, part_dk, part_dv)
    return tuple(a.reshape(B, HL, B) for a in grads)


def solution(mesh):
    nz = mesh.shape["ctx"] // NY
    tokens = P("ctx", "head", None)
    in_specs = (
        (tokens,) * 3 + (P("head", "ctx"), P("head", None)) + (tokens,) * 4 + (P("ctx", None), P("ctx"))
    )
    return jax.shard_map(
        functools.partial(local, nz, mesh.shape["head"]),
        mesh=mesh,
        in_specs=in_specs,
        out_specs=(tokens,) * 6,
        check_vma=False,
    )
```

time: 143 us -> 131 us (0.916)
  Pallas kernels: 141 us -> 130 us
    pallas_call x2 -> x1, Pallas kernels: 137 us -> 127 us  [fused(): pl.pallas_call(functools.partial(fused_kernel, nz, nh), out_shape=(low,)...]
where the time goes in v3:
time: 131 us
  Pallas kernels  130 us (99%)
    pallas_call x1, Pallas kernels, fused(): pl.pallas_call(functools.partial(fused_kernel, nz, nh), out_shape=(low,)...  127 us
    pallas_call x1, Pallas kernels, last(): pl.pallas_call(last_kernel, out_shape=(jax.ShapeDtypeStruct((HL * B, B),...  2.8 us

profile of v3, /device:TPU:32, one launch (start us, length us, event | category | flops | bytes accessed | tf_op | source)
XLA Modules:
  0.0 130.9 jit_solution(4713770998211649464)
XLA Ops:
  1.3 126.8 %shard_map.154 = (bf16[4,128,128]{2,1,0:T(8,128)(2,1)}, bf16[4,128,128]{2,1,0:T(8,128)(2,1)}, bf16[4,128,128]{2,1,0:T(8,128)(2,1)}, bf16[4,128,128]{2,1,0:T(8,12...) custom-call(s32[1,16]{1,0:T(1,128)} %lists.1, ...), custom_call_target="tpu_custom_call" | custom-call | tf_op jit(solution)/shard_map/pallas_call | solution.py:718
  128.1 2.8 %shard_map.155 = (bf16[512,128]{1,0:T(8,128)(2,1)}, bf16[512,128]{1,0:T(8,128)(2,1)}, bf16[512,128]{1,0:T(8,128)(2,1)}, bf16[512,128]{1,0:T(8,128)(2,1)}, bf16[5...) custom-call(bf16[4,3,128,128]{3,2,1,0:T(8,128)(2,1)} %get-tuple-element.20.lin, f32[4,128]{1,0:T(4,128)} %dec.3, ...), custom_call_target="tpu_custom_call" | custom-call | tf_op jit(solution)/shard_map/pallas_call | solution.py:795

commit v4 on v3

--- a/solution.py
+++ b/solution.py
@@ -11,7 +11,6 @@
 HL = 4
 B = 128
 NSEL = 16
-FR = 48
 EPS = 1e-05
 SCALE = 128 ** (-0.5)
 NEG = -1e30
@@ -285,8 +284,8 @@
     tmp,
     ring_s,
     ring_r,
-    bun_s,
-    bun_r,
+    opp_s,
+    opp_r,
     up_s,
     dn_s,
     col_r,
@@ -351,85 +350,62 @@
             head,
         )
 
-    def bundle(a, zz, h):
-        return pairs.at[zz, h, pl.ds(0, 3), a, pl.ds(FR, B - FR)]
-
-    def bundle_on(a, zz, h):
-        ref = bundle(a, zz, h)
-        start_remote(ref, ref, bun_s.at[a, zz, h - 2], bun_r.at[a, zz, h - 2], to_next(h), head)
-
-    def cell(a, zz, h, slot, rows):
-        return pairs.at[zz, h, slot, a, pl.ds(0, rows)]
-
-    def column_on(a, zz, h, up, dn, rows):
-        start_remote(up, cell(a, zz, h, 0, rows), up_s.at[a, zz, h], col_r.at[a, zz, h, 0], above, head)
-        start_remote(dn, cell(a, zz, h, 1, rows), dn_s.at[a, zz, h], col_r.at[a, zz, h, 1], below, head)
-
-    def rows_of(h):
-        return B if h < 2 else FR
+    def opposite(a, zz, h):
+        return pairs.at[zz, h, 2, a]
+
+    def opposite_on(a, zz, h):
+        ref = opposite(a, zz, h)
+        start_remote(ref, ref, opp_s.at[a, zz, h], opp_r.at[a, zz, h], to_next(h), head)
+
+    def opposite_wait(a, zz, h):
+        wait_recv(opposite(a, zz, h), opp_r.at[a, zz, h], me, head)
+
+    def column_on(a, zz, h, up, dn):
+        start_remote(up, pairs.at[zz, h, 0, a], up_s.at[a, zz, h], col_r.at[a, zz, h, 0], above, head)
+        start_remote(dn, pairs.at[zz, h, 1, a], dn_s.at[a, zz, h], col_r.at[a, zz, h, 1], below, head)
+
+    def column_wait(a, zz, h):
+        for k in (0, 1):
+            wait_recv(pairs.at[zz, h, k, a], col_r.at[a, zz, h, k], me, head)
 
     def begin(a):
-        def column_own(h):
-            column_on(a, z, h, own.at[h, part_up, a], own.at[h, part_dn, a], B)
-
-        for h in (0, 1):
+        for h in range(HL):
+            column_on(a, z, h, own.at[h, part_up, a], own.at[h, part_dn, a])
             ring_on(a, z, h, own.at[h, pl.ds(0, 2), a])
-        for h in (2, 3):
-            column_own(h)
-        for h in (2, 3):
-            ring_on(a, z, h, own.at[h, pl.ds(0, 2), a])
-        for h in (0, 1):
-            column_own(h)
-
-    def relay(a, zz, h, rows):
-        for k in (0, 1):
-            wait_recv(cell(a, zz, h, k, rows), col_r.at[a, zz, h, k], me, head)
+
+    def relay(a, h):
+        column_wait(a, z, h)
 
         @pl.when(inner_row)
         def _():
             for k, to in ((0, above), (1, below)):
                 start_remote(
-                    cell(a, zz, h, k, rows),
-                    cell(a, zz, h, 2, rows),
-                    rel_s.at[a, zz, h, k],
-                    col_r.at[a, zz, h, 2],
-                    to,
-                    head,
+                    pairs.at[z, h, k, a], opposite(a, z, h), rel_s.at[a, h, k], opp_r.at[a, z, h], to, head
                 )
 
-    def opposite(a, zz, h, rows):
-        wait_recv(cell(a, zz, h, 2, rows), col_r.at[a, zz, h, 2], me, head)
-
-    def lap(a, s, first=False, second=False, last=False):
+    def settle(a, s, last=False):
+        for h in range(HL):
+            opposite_wait(a, at(s, h), h)
+            if not last:
+                opposite_on(a, at(s, h), h)
+        for h in range(HL):
+            column_wait(a, at(s, h), h)
+
+    def lap(a, s, first=False, last=False):
         for h in range(HL):
             zz = at(s, h)
             wait_recv(ring(a, zz, h), ring_r.at[a, zz, h], me, head)
             if not last:
                 ring_on(a, zz, h)
-            rows = rows_of(h)
-            column_on(a, zz, h, cell(a, zz, h, 3 + part_up, rows), cell(a, zz, h, 3 + part_dn, rows), rows)
+            column_on(a, zz, h, pairs.at[zz, h, 3 + part_up, a], pairs.at[zz, h, 3 + part_dn, a])
         if first:
-            for h in (2, 3):
-                relay(a, z, h, B)
-            for h in (2, 3):
-                opposite(a, z, h, B)
-                bundle_on(a, z, h)
-            for h in (0, 1):
-                relay(a, z, h, B)
+            for h in range(HL):
+                relay(a, h)
+            for h in range(HL):
+                opposite_wait(a, z, h)
+                opposite_on(a, z, h)
         else:
-            for h in range(HL):
-                relay(a, at(s - 1, h), h, rows_of(h))
-        for h in (2, 3):
-            zz = at(s, h)
-            wait_recv(bundle(a, zz, h), bun_r.at[a, zz, h - 2], me, head)
-            if not last:
-                bundle_on(a, zz, h)
-        if second:
-            for h in (0, 1):
-                opposite(a, z, h, B)
-        elif not first:
-            for h in range(HL):
-                opposite(a, at(s - 2, h), h, rows_of(h))
+            settle(a, s - 1)
 
     lane = lax.broadcasted_iota(jnp.int32, (1, B), 1)
     causal = iota(0) >= iota(1)
@@ -504,9 +480,11 @@
     lap(0, 1, first=True)
     small_start(nz, head, fin_own, fin, fsem)
     scan_start(nz, head, state, fwd)
-    lap(0, 2, second=True)
     for h in range(HL):
         score(z, h, False)
+    lap(0, 2)
+    for h in range(HL):
+        score(at(1, h), h, True)
     small_rows(nz, head, fin_own, fin, fsem)
     scan_rows(nz, head, state, fin, fwd, False)
 
@@ -514,20 +492,16 @@
     def _(s):
         lap(0, s)
         for h in range(HL):
-            score(at(s - 2, h), h, True)
+            score(at(s - 1, h), h, True)
 
     begin(1)
     lap(0, nz - 1, last=True)
     for h in range(HL):
-        score(at(nz - 3, h), h, True)
-    for h in range(HL):
-        relay(0, at(nz - 1, h), h, rows_of(h))
+        score(at(nz - 2, h), h, True)
     lap(1, 1, first=True)
-    for s in (nz - 2, nz - 1):
-        for h in range(HL):
-            opposite(0, at(s, h), h, rows_of(h))
-        for h in range(HL):
-            score(at(s, h), h, True)
+    settle(0, nz - 1, last=True)
+    for h in range(HL):
+        score(at(nz - 1, h), h, True)
     lse_own[...] = jnp.zeros_like(lse_own)
     for h in range(HL):
         lse = mx[h] + jnp.log(jnp.sum(ls[h], axis=1, keepdims=True))
@@ -536,7 +510,7 @@
     small_start(nz, head, lse_own, lse_all, lsem)
     small_finish(nz, head, fin_own, fin, fsem)
     scan_spread(nz, head, fin, state_in, fwd, False)
-    lap(1, 2, second=True)
+    lap(1, 2)
     small_rows(nz, head, lse_own, lse_all, lsem)
     for h in range(HL):
         p = jnp.where(causal, jnp.exp(mm_t(own[h, 1, 0], own[h, 0, 0]) * SCALE - lcol[h]), 0.0)
@@ -546,12 +520,13 @@
         low = p.astype(BF16)
         acc[1, h] = mm(low, own[h, 0, 1])
         acc[0, h] = t_mm(low, own[h, 1, 1])
-    lap(1, 3)
+    lap(1, 3, last=nz == 4)
     small_finish(nz, head, lse_own, lse_all, lsem)
     for h in range(HL):
         weigh(z, h, False)
-    for h in range(HL):
-        weigh(at(1, h), h, True)
+    for s in (1, 2):
+        for h in range(HL):
+            weigh(at(s, h), h, True)
 
     def heads_start(k):
         for d in range(1, nh):
@@ -570,7 +545,7 @@
     if nz > 4:
         lap(1, 4)
         for h in range(HL):
-            weigh(at(2, h), h, True)
+            weigh(at(3, h), h, True)
 
     scan_finish(nz, head, state_in, fwd)
     squares = jnp.zeros((B, 1), F32)
@@ -590,18 +565,14 @@
         def _(s):
             lap(1, s)
             for h in range(HL):
-                weigh(at(s - 2, h), h, True)
+                weigh(at(s - 1, h), h, True)
 
         lap(1, nz - 1, last=True)
         for h in range(HL):
-            weigh(at(nz - 3, h), h, True)
-    for h in range(HL):
-        relay(1, at(nz - 1, h), h, rows_of(h))
-    for s in (nz - 2, nz - 1):
-        for h in range(HL):
-            opposite(1, at(s, h), h, rows_of(h))
-        for h in range(HL):
-            weigh(at(s, h), h, True)
+            weigh(at(nz - 2, h), h, True)
+    settle(1, nz - 1, last=True)
+    for h in range(HL):
+        weigh(at(nz - 1, h), h, True)
 
     partial = jnp.zeros((B, 1), F32)
     for h in range(HL):
@@ -684,26 +655,25 @@
 
     for a in range(2):
 
-        def column_left(zz, h, rows):
-            wait_send(cell(a, zz, h, 0, rows), up_s.at[a, zz, h], me, head)
-            wait_send(cell(a, zz, h, 1, rows), dn_s.at[a, zz, h], me, head)
+        def column_left(zz, h):
+            wait_send(pairs.at[zz, h, 0, a], up_s.at[a, zz, h], me, head)
+            wait_send(pairs.at[zz, h, 1, a], dn_s.at[a, zz, h], me, head)
+
+        for h in range(HL):
+            column_left(z, h)
 
             @pl.when(inner_row)
             def _():
                 for k in (0, 1):
-                    wait_send(cell(a, zz, h, k, rows), rel_s.at[a, zz, h, k], me, head)
-
-        for h in range(HL):
-            column_left(z, h, B)
+                    wait_send(pairs.at[z, h, k, a], rel_s.at[a, h, k], me, head)
 
         @pl.loop(0, nz - 1)
         def _(s):
             for h in range(HL):
                 zz = at(s, h)
                 wait_send(ring(a, zz, h), ring_s.at[a, zz, h], me, head)
-                if h >= 2:
-                    wait_send(bundle(a, zz, h), bun_s.at[a, zz, h - 2], me, head)
-                column_left(at(s + 1, h), h, rows_of(h))
+                wait_send(opposite(a, zz, h), opp_s.at[a, zz, h], me, head)
+                column_left(at(s + 1, h), h)
 
 
 def fused(nz, nh, lists, counts, arrays, decay, gain):
@@ -749,12 +719,12 @@
             pltpu.VMEM((HL * B, B), F32),
             sem((2, nz, HL)),
             sem((2, nz, HL)),
-            sem((2, nz, 2)),
-            sem((2, nz, 2)),
             sem((2, nz, HL)),
             sem((2, nz, HL)),
-            sem((2, nz, HL, 3)),
+            sem((2, nz, HL)),
+            sem((2, nz, HL)),
             sem((2, nz, HL, 2)),
+            sem((2, HL, 2)),
             sem((5, max(nz, NY))),
             sem((5, max(nz, NY))),
             sem((5, max(nz, NY))),

time: 131 us -> 121 us (0.924)
  Pallas kernels: 130 us -> 120 us
    pallas_call x1, Pallas kernels: 127 us -> 117 us  [fused(): pl.pallas_call(functools.partial(fused_kernel, nz, nh), out_shape=(low,)...]
where the time goes in v4:
time: 121 us
  Pallas kernels  120 us (99%)
  between operations  1.29 us (1%)
    pallas_call x1, Pallas kernels, fused(): pl.pallas_call(functools.partial(fused_kernel, nz, nh), out_shape=(low,)...  117 us
    pallas_call x1, Pallas kernels, last(): pl.pallas_call(last_kernel, out_shape=(jax.ShapeDtypeStruct((HL * B, B),...  2.8 us

profile of v4, /device:TPU:32, one launch (start us, length us, event | category | flops | bytes accessed | tf_op | source)
XLA Modules:
  0.0 120.9 jit_solution(15615186048010233378)
XLA Ops:
  1.3 116.9 %shard_map.154 = (bf16[4,128,128]{2,1,0:T(8,128)(2,1)}, bf16[4,128,128]{2,1,0:T(8,128)(2,1)}, bf16[4,128,128]{2,1,0:T(8,128)(2,1)}, bf16[4,128,128]{2,1,0:T(8,12...) custom-call(s32[1,16]{1,0:T(1,128)} %lists.1, ...), custom_call_target="tpu_custom_call" | custom-call | tf_op jit(solution)/shard_map/pallas_call | solution.py:688
  118.2 2.8 %shard_map.155 = (bf16[512,128]{1,0:T(8,128)(2,1)}, bf16[512,128]{1,0:T(8,128)(2,1)}, bf16[512,128]{1,0:T(8,128)(2,1)}, bf16[512,128]{1,0:T(8,128)(2,1)}, bf16[5...) custom-call(bf16[4,3,128,128]{3,2,1,0:T(8,128)(2,1)} %get-tuple-element.20.lin, f32[4,128]{1,0:T(4,128)} %dec.3, ...), custom_call_target="tpu_custom_call" | custom-call | tf_op jit(solution)/shard_map/pallas_call | solution.py:765

commit v5 on v4

--- a/solution.py
+++ b/solution.py
@@ -61,6 +61,10 @@
     return jnp.where(lax.rem(y + NY - 1, NY) == r, 0, jnp.where(lax.rem(y + 1, NY) == r, 1, 2))
 
 
+def far_first(n):
+    return sorted(range(1, n), key=lambda d: (-min(d, n - d), d))
+
+
 def place(nz):
     own = lax.axis_index("ctx")
     return own // nz, lax.rem(own, nz)
@@ -89,11 +93,12 @@
     return [
         pltpu.VMEM((nz, rs, B), BF16),
         pltpu.VMEM((nz, rs, B), F32),
-        pltpu.VMEM((NY, rs, B), F32),
+        pltpu.VMEM((NY, rs, B), BF16),
+        pltpu.VMEM((rs, B), BF16),
+        pltpu.VMEM((nz, rs, B), BF16),
+        pltpu.SemaphoreType.DMA((6, max(nz, NY))),
+        pltpu.SemaphoreType.DMA((2,)),
         pltpu.VMEM((rs, B), F32),
-        pltpu.VMEM((nz, rs, B), BF16),
-        pltpu.SemaphoreType.DMA((6, nz)),
-        pltpu.SemaphoreType.DMA((2,)),
     ]
 
 
@@ -101,7 +106,7 @@
     zbuf, sems, lsem = bufs[0], bufs[5], bufs[6]
     rs = HL * B // nz
     y, z = place(nz)
-    for d in range(1, nz):
+    for d in far_first(nz):
         zz = lax.rem(z + d, nz)
         start_remote(
             local.at[pl.ds(zz * rs, rs)], zbuf.at[z], sems.at[0, zz], sems.at[1, z], y * nz + zz, head
@@ -110,7 +115,7 @@
 
 
 def scan_rows(nz, head, local, fin, bufs, reverse):
-    zbuf, ebuf, tbuf, tsrc, _, sems, lsem = bufs
+    zbuf, ebuf, tbuf, tsrc, _, sems, lsem, _ = bufs
     rs = HL * B // nz
     y, z = place(nz)
     own = y * nz + z
@@ -125,38 +130,51 @@
         m = nz - 1 - lap if reverse else lap
         ebuf[m] = total
         total = total * jnp.exp(fin[y, m, pl.ds(hz, 1), :]) + zbuf[m].astype(F32)
-    tsrc[...] = total
-    for d in range(1, NY):
-        yy = lax.rem(y + d, NY)
-        start_remote(tsrc, tbuf.at[y], sems.at[2, yy], sems.at[3, y], yy * nz + z, head)
+    tsrc[...] = total.astype(BF16)
+    for yy in range(NY):
+
+        @pl.when((yy < y) if reverse else (yy > y))
+        def _():
+            start_remote(tsrc, tbuf.at[y], sems.at[2, yy], sems.at[3, y], yy * nz + z, head)
+
     for d in range(1, nz):
         zz = lax.rem(z + d, nz)
         wait_send(zbuf.at[0], sems.at[0, zz], own, head)
 
 
 def scan_spread(nz, head, fin, out, bufs, reverse):
-    _, ebuf, tbuf, tsrc, sbuf, sems, lsem = bufs
+    _, ebuf, tbuf, tsrc, sbuf, sems, lsem, cbuf = bufs
     rs = HL * B // nz
     y, z = place(nz)
     own = y * nz + z
     hz = z * rs // B
-    for d in range(1, NY):
-        yy = lax.rem(y + d, NY)
-        wait_recv(tbuf.at[yy], sems.at[3, yy], own, head)
-        wait_send(tsrc, sems.at[2, yy], own, head)
-    carry = jnp.zeros((rs, B), F32)
+    for yy in range(NY):
+
+        @pl.when((yy > y) if reverse else (yy < y))
+        def _():
+            wait_recv(tbuf.at[yy], sems.at[3, yy], own, head)
+
+        @pl.when((yy < y) if reverse else (yy > y))
+        def _():
+            wait_send(tsrc, sems.at[2, yy], own, head)
+
+    cbuf[...] = jnp.zeros_like(cbuf)
     for lap in range(NY):
         r = NY - 1 - lap if reverse else lap
-        use = (r > y) if reverse else (r < y)
-        span = jnp.zeros((1, B), F32)
-        for m in range(nz):
-            span = span + fin[r, m, pl.ds(hz, 1), :]
-        carry = jnp.where(use, carry * jnp.exp(span) + tbuf[r], carry)
+
+        @pl.when((r > y) if reverse else (r < y))
+        def _():
+            span = jnp.zeros((1, B), F32)
+            for m in range(nz):
+                span = span + fin[r, m, pl.ds(hz, 1), :]
+            cbuf[...] = cbuf[...] * jnp.exp(span) + tbuf[r].astype(F32)
+
+    carry = cbuf[...]
     for lap in range(nz):
         m = nz - 1 - lap if reverse else lap
         sbuf[m] = (ebuf[m] + carry).astype(BF16)
         carry = carry * jnp.exp(fin[y, m, pl.ds(hz, 1), :])
-    for d in range(1, nz):
+    for d in far_first(nz):
         zz = lax.rem(z + d, nz)
         start_remote(
             sbuf.at[zz], out.at[pl.ds(z * rs, rs)], sems.at[4, zz], sems.at[5, z], y * nz + zz, head
@@ -178,7 +196,7 @@
 
 def small_start(nz, head, src, dst, sems):
     y, z = place(nz)
-    for d in range(1, nz):
+    for d in far_first(nz):
         zz = lax.rem(z + d, nz)
         start_remote(src, dst.at[y, z], sems.at[0, zz], sems.at[1, z], y * nz + zz, head)
     pltpu.make_async_copy(src, dst.at[y, z], sems.at[2, 0]).start()
@@ -282,6 +300,7 @@
     hbuf,
     hsrc,
     tmp,
+    query_t,
     ring_s,
     ring_r,
     opp_s,
@@ -300,7 +319,6 @@
     head = lax.axis_index("head")
     y, z = place(nz)
     me = y * nz + z
-    n = NY * nz
     right, left = y * nz + lax.rem(z + 1, nz), y * nz + lax.rem(z + nz - 1, nz)
     above, below = lax.rem(y + 1, NY) * nz + z, lax.rem(y + NY - 1, NY) * nz + z
     part_up = jnp.where(y < NY - 1, 0, 1)
@@ -327,8 +345,6 @@
 
     heads(sk, own_at(0, 0))
     heads(sq, own_at(1, 0))
-    heads(sv, own_at(0, 1))
-    heads(og, own_at(1, 1))
     greeted(nz, nh)
 
     def at(s, h):
@@ -391,13 +407,15 @@
         for h in range(HL):
             column_wait(a, at(s, h), h)
 
-    def lap(a, s, first=False, last=False):
+    def lap(a, s, first=False, last=False, mid=None):
         for h in range(HL):
             zz = at(s, h)
             wait_recv(ring(a, zz, h), ring_r.at[a, zz, h], me, head)
             if not last:
                 ring_on(a, zz, h)
             column_on(a, zz, h, pairs.at[zz, h, 3 + part_up, a], pairs.at[zz, h, 3 + part_dn, a])
+        if mid is not None:
+            mid()
         if first:
             for h in range(HL):
                 relay(a, h)
@@ -449,25 +467,30 @@
 
     begin(0)
 
-    for h in range(HL):
-        s = jnp.where(causal, mm_t(own[h, 1, 0], own[h, 0, 0]) * SCALE, NEG)
-        m = jnp.broadcast_to(jnp.max(s, axis=1, keepdims=True), (B, B))
-        mx[h] = m
-        ls[h] = jnp.exp(s - m)
-    column = lax.broadcasted_iota(jnp.int32, (nz, B), 0)
-    named = jnp.zeros((1, B), F32)
-    for e in range(NSEL):
-        named = jnp.where((lane == lists[0, e]) & (e < count[0]), 1.0, named)
-    for k, off in ((0, NY - 1), (1, 1), (2, 2), (3, 0)):
-        block = lax.rem(y + off, NY) * nz + column
-        b = jnp.full((nz, B), NEG, F32)
-        for e in range(NSEL):
-            b = jnp.where((block == lists[0, e]) & (e < count[0]), 0.0, b)
-        bias[k] = b
+    def start_scores():
+        for h in range(HL):
+            s = jnp.where(causal, mm_t(own[h, 1, 0], own[h, 0, 0]) * SCALE, NEG)
+            m = jnp.broadcast_to(jnp.max(s, axis=1, keepdims=True), (B, B))
+            mx[h] = m
+            ls[h] = jnp.exp(s - m)
+        column = lax.broadcasted_iota(jnp.int32, (nz, B), 0)
+        for k, off in ((0, NY - 1), (1, 1), (2, 2), (3, 0)):
+            block = lax.rem(y + off, NY) * nz + column
+            b = jnp.full((nz, B), NEG, F32)
+            for e in range(NSEL):
+                b = jnp.where((block == lists[0, e]) & (e < count[0]), 0.0, b)
+            bias[k] = b
+
+    lap(0, 1, first=True, mid=start_scores)
+    heads(sv, own_at(0, 1))
+    heads(og, own_at(1, 1))
     heads(lk, lin_at(1))
     heads(lv, lin_at(2))
     heads(lq, lin_at(0))
     run = running_of(dec[...])
+    named = jnp.zeros((1, B), F32)
+    for e in range(NSEL):
+        named = jnp.where((lane == lists[0, e]) & (e < count[0]), 1.0, named)
     finish = run[:, B - 1 : B]
     fin_own[...] = jnp.concatenate(
         [jnp.broadcast_to(finish, (HL, B)), named, jnp.zeros((HL - 1, B), F32)], axis=0
@@ -476,29 +499,36 @@
     for h in range(HL):
         k = lin[h, 1].astype(F32) * col_of(trailing[h : h + 1])
         state[pl.ds(h * B, B), :] = t_mm(k.astype(BF16), lin[h, 2]).astype(BF16)
-
-    lap(0, 1, first=True)
     small_start(nz, head, fin_own, fin, fsem)
     scan_start(nz, head, state, fwd)
     for h in range(HL):
         score(z, h, False)
     lap(0, 2)
-    for h in range(HL):
+    for h in (0, 1):
         score(at(1, h), h, True)
     small_rows(nz, head, fin_own, fin, fsem)
     scan_rows(nz, head, state, fin, fwd, False)
 
     @pl.loop(3, nz - 1)
     def _(s):
-        lap(0, s)
-        for h in range(HL):
+        def rest():
+            for h in (2, 3):
+                score(at(s - 2, h), h, True)
+
+        lap(0, s, mid=rest)
+        for h in (0, 1):
             score(at(s - 1, h), h, True)
 
     begin(1)
-    lap(0, nz - 1, last=True)
-    for h in range(HL):
+
+    def rest(s):
+        for h in (2, 3):
+            score(at(s, h), h, True)
+
+    lap(0, nz - 1, last=True, mid=lambda: rest(nz - 3))
+    for h in (0, 1):
         score(at(nz - 2, h), h, True)
-    lap(1, 1, first=True)
+    lap(1, 1, first=True, mid=lambda: rest(nz - 2))
     settle(0, nz - 1, last=True)
     for h in range(HL):
         score(at(nz - 1, h), h, True)
@@ -544,7 +574,7 @@
 
     if nz > 4:
         lap(1, 4)
-        for h in range(HL):
+        for h in (0, 1):
             weigh(at(3, h), h, True)
 
     scan_finish(nz, head, state_in, fwd)
@@ -555,6 +585,7 @@
         w = (mm_t(lin[h, 0], lin[h, 1]) * within_of(row, col)).astype(BF16)
         o = mm(w, lin[h, 2]) + jnp.exp(col) * mm(lin[h, 0], state_in[pl.ds(h * B, B), :])
         lo[h] = o
+        query_t[h] = jnp.transpose(lin[h, 0].astype(F32) * jnp.exp(col)).astype(BF16)
         squares = squares + jnp.sum(o * o, axis=1, keepdims=True)
     hsrc[0] = jnp.broadcast_to(row_of(squares), (8, B))
     heads_start(0)
@@ -563,13 +594,18 @@
 
         @pl.loop(5, nz - 1)
         def _(s):
-            lap(1, s)
-            for h in range(HL):
+            def rest():
+                for h in (2, 3):
+                    weigh(at(s - 2, h), h, True)
+
+            lap(1, s, mid=rest)
+            for h in (0, 1):
                 weigh(at(s - 1, h), h, True)
 
         lap(1, nz - 1, last=True)
-        for h in range(HL):
-            weigh(at(nz - 2, h), h, True)
+        for s, some in ((nz - 3, (2, 3)), (nz - 2, range(HL))):
+            for h in some:
+                weigh(at(s, h), h, True)
     settle(1, nz - 1, last=True)
     for h in range(HL):
         weigh(at(nz - 1, h), h, True)
@@ -595,40 +631,53 @@
         dkq[1, h] = mm(ds, own[h, 0, 0])
         dkq[0, h] = t_mm(ds, own[h, 1, 0])
 
-    def key_grads(lo_i, hi_i):
-        @pl.loop(lo_i, jnp.minimum(hi_i, me))
-        def _(i):
-            r, zz = i // nz, lax.rem(i, nz)
-            k = jnp.where(r == y, 3, slot_of(r, y))
+    def row_grads(k, off, keys):
+        r = lax.rem(y + off, NY)
+        t = 1 if keys else 0
+
+        @pl.when((r < y) if keys else (r > y))
+        def _():
+            @pl.loop(0, nz // 4)
+            def _(c):
+                for h in range(HL):
+                    parts, rows = [], []
+                    for i in range(4):
+                        zz = 4 * c + i
+                        delta = dcol[h] if keys else del_all[r, zz, h : h + 1, :]
+                        parts.append((a1[zz, h, k] * (a2[zz, h, k] - delta)).astype(BF16))
+                        rows.append(pairs[zz, h, k, 0])
+                    dkq[t, h] = dkq[t, h] + mm(jnp.concatenate(parts, axis=1), jnp.concatenate(rows, axis=0))
+
+    def near_grads(keys):
+        @pl.loop(0 if keys else z + 1, z if keys else nz)
+        def _(zz):
             for h in range(HL):
-                ds = (a1[zz, h, k] * (a2[zz, h, k] - dcol[h])).astype(BF16)
-                dkq[1, h] = dkq[1, h] + mm(ds, pairs[zz, h, k, 0])
-
-    def query_grads(lo_i, hi_i):
-        @pl.loop(jnp.maximum(lo_i, me + 1), hi_i)
-        def _(i):
-            r, zz = i // nz, lax.rem(i, nz)
-            k = jnp.where(r == y, 3, slot_of(r, y))
-            slot = jnp.where(r == y, 4, k)
-            for h in range(HL):
-                ds = (a1[zz, h, k] * (a2[zz, h, k] - del_all[r, zz, h : h + 1, :])).astype(BF16)
-                dkq[0, h] = dkq[0, h] + mm(ds, pairs[zz, h, slot, 0])
+                delta = dcol[h] if keys else del_all[y, zz, h : h + 1, :]
+                ds = (a1[zz, h, 3] * (a2[zz, h, 3] - delta)).astype(BF16)
+                t, slot = (1, 3) if keys else (0, 4)
+                dkq[t, h] = dkq[t, h] + mm(ds, pairs[zz, h, slot, 0])
 
     width = HL * nh * B
     root = jnp.sqrt(heads_total(0) / width + EPS)
+    inv = col_of(1.0 / root)
+    for h in range(HL):
+        cot[h] = cot[h] * inv
+    cube = 1.0 / (width * root * root * root)
     inner = heads_total(1)
-    factor = col_of(inner / (width * root * root * root))
-    inv = col_of(1.0 / root)
-    leading = jnp.exp(run)
-    for h in range(HL):
-        lc = cot[h] * inv - lo[h] * factor
+    factor = col_of(inner * cube)
+    for h in range(HL):
+        lc = cot[h] - lo[h] * factor
         cot[h] = lc
-        q = (lin[h, 0].astype(F32) * col_of(leading[h : h + 1])).astype(BF16)
-        state[pl.ds(h * B, B), :] = t_mm(q, lc.astype(BF16)).astype(BF16)
+        state[pl.ds(h * B, B), :] = mm(query_t[h], lc.astype(BF16)).astype(BF16)
     scan_start(nz, head, state, bwd)
-    key_grads(0, n // 2)
+    row_grads(0, NY - 1, True)
     small_rows(nz, head, del_own, del_all, dsem)
+    near_grads(True)
+    row_grads(1, 1, True)
     scan_rows(nz, head, state, fin, bwd, True)
+    near_grads(False)
+    row_grads(2, 2, True)
+    scan_spread(nz, head, fin, rev_out, bwd, True)
     for h in range(HL):
         row = run[h : h + 1]
         col = col_of(row)
@@ -641,9 +690,8 @@
         part_dk[h] = t_mm(pair, lin[h, 0])
         part_dv[h] = t_mm(w, c)
     small_finish(nz, head, del_own, del_all, dsem)
-    scan_spread(nz, head, fin, rev_out, bwd, True)
-    key_grads(n // 2, n)
-    query_grads(0, n)
+    for k, off in ((0, NY - 1), (1, 1), (2, 2)):
+        row_grads(k, off, False)
     for h in range(HL):
         dk_out[h] = (dkq[0, h] * SCALE).astype(BF16)
         dq_out[h] = (dkq[1, h] * SCALE).astype(BF16)
@@ -717,6 +765,7 @@
             pltpu.VMEM((2, nh, 8, B), F32),
             pltpu.VMEM((2, 8, B), F32),
             pltpu.VMEM((HL * B, B), F32),
+            pltpu.VMEM((HL, B, B), BF16),
             sem((2, nz, HL)),
             sem((2, nz, HL)),
             sem((2, nz, HL)),

time: 121 us -> 120 us (level)
  Pallas kernels: 120 us -> 118 us
    pallas_call x1, Pallas kernels: 117 us -> 116 us  [fused(): pl.pallas_call(functools.partial(fused_kernel, nz, nh), out_shape=(low,)...]
where the time goes in v5:
time: 120 us
  Pallas kernels  118 us (98%)
  between operations  1.29 us (1%)
    pallas_call x1, Pallas kernels, fused(): pl.pallas_call(functools.partial(fused_kernel, nz, nh), out_shape=(low,)...  116 us
    pallas_call x1, Pallas kernels, last(): pl.pallas_call(last_kernel, out_shape=(jax.ShapeDtypeStruct((HL * B, B),...  2.8 us

profile of v5, /device:TPU:32, one launch (start us, length us, event | category | flops | bytes accessed | tf_op | source)
XLA Modules:
  0.0 119.7 jit_solution(4126159168432975681)
XLA Ops:
  1.3 115.6 %shard_map.154 = (bf16[4,128,128]{2,1,0:T(8,128)(2,1)}, bf16[4,128,128]{2,1,0:T(8,128)(2,1)}, bf16[4,128,128]{2,1,0:T(8,128)(2,1)}, bf16[4,128,128]{2,1,0:T(8,12...) custom-call(s32[1,16]{1,0:T(1,128)} %lists.1, ...), custom_call_target="tpu_custom_call" | custom-call | tf_op jit(solution)/shard_map/pallas_call | solution.py:736
  116.9 2.8 %shard_map.155 = (bf16[512,128]{1,0:T(8,128)(2,1)}, bf16[512,128]{1,0:T(8,128)(2,1)}, bf16[512,128]{1,0:T(8,128)(2,1)}, bf16[512,128]{1,0:T(8,128)(2,1)}, bf16[5...) custom-call(bf16[4,3,128,128]{3,2,1,0:T(8,128)(2,1)} %get-tuple-element.20.lin, f32[4,128]{1,0:T(4,128)} %dec.3, ...), custom_call_target="tpu_custom_call" | custom-call | tf_op jit(solution)/shard_map/pallas_call | solution.py:814

commit v6 on v5

--- a/solution.py
+++ b/solution.py
@@ -606,8 +606,9 @@
         for s, some in ((nz - 3, (2, 3)), (nz - 2, range(HL))):
             for h in some:
                 weigh(at(s, h), h, True)
-    settle(1, nz - 1, last=True)
-    for h in range(HL):
+    for h in range(HL):
+        opposite_wait(1, at(nz - 1, h), h)
+        column_wait(1, at(nz - 1, h), h)
         weigh(at(nz - 1, h), h, True)
 
     partial = jnp.zeros((B, 1), F32)

time: 120 us -> 120 us (level)
  no operation moved by 1% of the time
where the time goes in v6:
time: 120 us; the launch traced here: 119 us
  Pallas kernels  118 us (98%)
  between operations  1.29 us (1%)
    pallas_call x1, Pallas kernels, fused(): pl.pallas_call(functools.partial(fused_kernel, nz, nh), out_shape=(low,)...  115 us
    pallas_call x1, Pallas kernels, last(): pl.pallas_call(last_kernel, out_shape=(jax.ShapeDtypeStruct((HL * B, B),...  2.8 us

profile of v6, /device:TPU:32, one launch (start us, length us, event | category | flops | bytes accessed | tf_op | source)
XLA Modules:
  0.0 119.3 jit_solution(16442133763590741527)
XLA Ops:
  1.3 115.2 %shard_map.154 = (bf16[4,128,128]{2,1,0:T(8,128)(2,1)}, bf16[4,128,128]{2,1,0:T(8,128)(2,1)}, bf16[4,128,128]{2,1,0:T(8,128)(2,1)}, bf16[4,128,128]{2,1,0:T(8,12...) custom-call(s32[1,16]{1,0:T(1,128)} %lists.1, ...), custom_call_target="tpu_custom_call" | custom-call | tf_op jit(solution)/shard_map/pallas_call | solution.py:737
  116.5 2.8 %shard_map.155 = (bf16[512,128]{1,0:T(8,128)(2,1)}, bf16[512,128]{1,0:T(8,128)(2,1)}, bf16[512,128]{1,0:T(8,128)(2,1)}, bf16[512,128]{1,0:T(8,128)(2,1)}, bf16[5...) custom-call(bf16[4,3,128,128]{3,2,1,0:T(8,128)(2,1)} %get-tuple-element.20.lin, f32[4,128]{1,0:T(4,128)} %dec.3, ...), custom_call_target="tpu_custom_call" | custom-call | tf_op jit(solution)/shard_map/pallas_call | solution.py:815
